TPU v7x, 32 devices: a whole 2x2x4 slice. The times are simulated.
32 devices in a mesh: depth: 4 (over x, core), tile: 8 (over z, y).
Axes of the slice: x: 2, y: 2, z: 4, core: 2. Of those that a mesh axis runs over, the one named last changes fastest.
Arguments:
- potential: float32 [3, 256, 256, 512], P(None, 'depth', 'tile'), may hold values from -6 to 6
- channel_index: int32 [64], replicated, may hold values from 0 to 63, each once
- patch_offsets: int32 [3], replicated, may hold values from 0 to 4095
Outputs:
- pol_spectra: float32 [64, 2, 256, 512], P('depth', None, 'tile')
- faraday_depth: float32 [256, 512], P('tile')
Inputs may be any that keep to these rules, and one draw needn't show every extreme that they name: `channel_index`: every channel index appears once.
All inputs are finite; a program needn't handle non-finite values.
Results may differ from a plain program's by a relative error of at most 0.00002.
Values sent between devices are 32-bit elements; how exact they have to be, the bound alone decides.
A program may use at most 256 MiB of HBM per device.

v0:
```python
import jax
import jax.numpy as jnp
from jax import lax
from jax.sharding import PartitionSpec as P

NCH = 64


two_pi = 6.283185307179586
faraday_coef = 0.25


def padded_2(block, sides, width):
    for axis, dim in sides:
        count = lax.axis_size(axis)
        forward = [(i, i + 1) for i in range(count - 1)]
        backward = [(target, source) for source, target in forward]
        low = lax.ppermute(
            lax.slice_in_dim(block, block.shape[dim] - width, None, axis=dim), axis, forward
        )
        high = lax.ppermute(lax.slice_in_dim(block, 0, width, axis=dim), axis, backward)
        block = jnp.concatenate([low, block, high], axis=dim)
    return block


def carried_in(part, axis, combine, identity):
    place = lax.axis_index(axis)
    gathered = lax.all_gather(part, axis)
    state = jnp.zeros_like(part) + jnp.asarray(identity, part.dtype)

    def one(lap, state):
        return combine(state, lax.dynamic_index_in_dim(gathered, lap, 0, False))

    return lax.fori_loop(0, place, one, state)


def deriv_lead(padded):
    return (8.0 * (padded[3:-1] - padded[1:-3]) - (padded[4:] - padded[:-4])) / 12.0


def deriv_mid(padded):
    return (8.0 * (padded[:, 3:-1] - padded[:, 1:-3]) - (padded[:, 4:] - padded[:, :-4])) / 12.0


def offset_last(values, step):
    zeros = jnp.zeros(values.shape[:-1] + (abs(step),), values.dtype)
    if step > 0:
        return jnp.concatenate([values[..., step:], zeros], axis=-1)
    return jnp.concatenate([zeros, values[..., :step]], axis=-1)


def deriv_last(values):
    return (
        8.0 * (offset_last(values, 1) - offset_last(values, -1))
        - (offset_last(values, 2) - offset_last(values, -2))
    ) / 12.0


def body(potential, channel_index, patch_offsets):
    depth_count = lax.axis_size("depth")
    slab, strip, width = (potential.shape[1], potential.shape[2], potential.shape[3])
    padded = padded_2(potential, (("depth", 1), ("tile", 2)), 2)
    along_z = padded[0:2, :, 2:-2]
    along_x = padded[1:3, 2:-2]
    field_x = deriv_last(potential[2]) - deriv_lead(along_z[1])
    field_y = deriv_lead(along_z[0]) - deriv_mid(along_x[1])
    field_z = deriv_mid(along_x[0]) - deriv_last(potential[0])
    zstart = lax.axis_index("depth") * slab
    xstart = lax.axis_index("tile") * strip
    zpos = (zstart + jnp.arange(slab, dtype=jnp.int32) + patch_offsets[0]).astype(jnp.float32)
    xpos = (xstart + jnp.arange(strip, dtype=jnp.int32) + patch_offsets[1]).astype(jnp.float32)
    ypos = (jnp.arange(width, dtype=jnp.int32) + patch_offsets[2]).astype(jnp.float32)
    density = (
        1.0
        + 0.5
        * jnp.cos(zpos * (two_pi / 61.0))[:, None, None]
        * jnp.cos(xpos * (two_pi / 37.0))[None, :, None]
        + 0.3 * jnp.sin(ypos * (two_pi / 53.0))[None, None, :]
    )
    stokes_q = density * (field_y * field_y - field_x * field_x)
    stokes_u = -2.0 * density * field_x * field_y
    slab_sums = jnp.cumsum(density * field_z, axis=0)
    own_total = faraday_coef * slab_sums[-1]
    nearer = carried_in(
        own_total, "depth", lambda early, late: early + late, jnp.zeros_like(own_total)
    )
    faraday_depth = lax.psum(own_total, "depth")
    rotation = faraday_coef * slab_sums + nearer[None]
    freq = 0.5 + 1.5 * channel_index.astype(jnp.float32) / (NCH - 1)
    lam2 = (0.2998 / freq) ** 2
    weight = 1.0 / (freq * jnp.sqrt(jnp.float32(slab * depth_count)))
    rows = NCH // depth_count
    blocks = lax.axis_size("depth") * rows // rows

    def one_block(pair):
        lam_block, weight_block = pair
        phase = 2.0 * lam_block[:, None, None, None] * rotation[None]
        cosine = jnp.cos(phase)
        sine = jnp.sin(phase)
        real_part = (
            jnp.sum(stokes_q[None] * cosine - stokes_u[None] * sine, axis=1)
            * weight_block[:, None, None]
        )
        imag_part = (
            jnp.sum(stokes_q[None] * sine + stokes_u[None] * cosine, axis=1)
            * weight_block[:, None, None]
        )
        return jnp.stack([real_part, imag_part], axis=1)

    stacked = lax.map(one_block, (lam2.reshape(blocks, rows), weight.reshape(blocks, rows)))
    pol_spectra = lax.psum_scatter(
        stacked.reshape(lax.axis_size("depth") * rows, 2, strip, width),
        "depth",
        scatter_dimension=0,
        tiled=True,
    )
    return (pol_spectra, faraday_depth)


def solution(mesh):
    in_specs = (P(None, "depth", "tile", None), P(), P())
    out_specs = (P("depth", None, "tile", None), P("tile", None))
    return jax.shard_map(body, mesh=mesh, in_specs=in_specs, out_specs=out_specs, check_vma=False)
```

profile of v0, /device:TPU:0, one launch (start us, length us, event | category | flops | bytes accessed | tf_op | source)
XLA Modules:
  0.0 1292.3 jit_solution(8987090101032574109)
XLA Ops:
  7.2 1.2 fusion.56
  8.4 2.4 collective-permute-start.1
  10.8 1.3 collective-permute-start
  12.1 6.8 slice_bitcast_fusion
  19.0 4.8 fusion.57
  23.8 4.8 fusion.58
  30.8 8.0 fusion.59
  38.7 1.0 constant_dynamic-update-slice_fusion.3
  39.7 13.0 %constant_dynamic-update-slice_fusion.1 = (f32[3,66,32,512]{3,2,1,0:T(8,128)S(1)}, f32[3,68,32,512]{3,2,1,0:T(8,128)}, f32[3,66,32,512]{3,2,1,0:T(8,128)}) fusion(f32[3,64,32,512]{3,2,1,0:T(8,128)} %param.7, f32[3,68,32,512]{3,2,1,0:T(8,128)} %get-tuple-element.119, f32[3,66,32,512]{3,2,1,0:T(8,128)} %get-tuple-element.118), kind=kLoop, calls=%fused_computation.76 | loop fusion | bytes 50331648
  53.6 9.0 fusion.55
  62.6 4.3 collective-permute-start.2
  66.9 1.5 collective-permute-start.3
  69.1 4.8 fusion.60
  73.9 28.4 %collective-permute-done.2 = f32[3,68,2,512]{3,2,1,0:T(2,128)S(1)} collective-permute-done((f32[3,68,2,512]{3,2,1,0:T(2,128)S(1)}, f32[3,68,2,512]{3,2,1,0:T(2,128)S(1)}, u32[]{:S(2)}, u32[]{:S(2)}) %collective-permute-start.2) | collective-permute-done | bytes 835616 | tf_op jit(solution)/shard_map/ppermute | solution.py:18
  102.3 10.6 fusion.11
  112.9 16.0 %fusion.12 = f32[64,32,512]{2,1,0:T(8,128)S(1)} fusion(f32[64,36,512]{2,1,0:T(8,128)} %get-tuple-element.95, f32[64,32,510]{2,1,0:T(8,128)} %get-tuple-element.111, f32[64,32,510]{2,1,0:T(8,128)} %get-tuple-element.110, f32[64,32,511]{2,1,0:T(8,128)} %get-tuple-element.109, f32[64,32,511]{2,1,0:T(8,128)} %get-tuple-element.108, ...), kind=kOutput, calls=%fused_computation.27 | output fusion | flops 79691776 | bytes 37758976 | tf_op jit(solution)/shard_map/jit(cumsum)/reduce_window_sum | solution.py:82
  128.9 1.9 copy-done.2
  131.5 7.5 all_gather.4
  139.0 5.1 multiply_add_fusion
  144.2 27.3 %fusion.14 = (f32[64,32,512]{2,1,0:T(8,128)}, f32[64,32,512]{2,1,0:T(8,128)S(1)}, f32[64,32,512]{2,1,0:T(8,128)S(1)}) fusion(f32[512]{0:T(512)S(1)} %sine_multiply_fusion, f32[64,32]{1,0:T(8,128)S(1)} %multiply_add_fusion.1, f32[64,36,512]{2,1,0:T(8,128)} %get-tuple-element.96, f32[3,66,32,512]{3,2,1,0:T(8,128)} %get-tuple-element.103, ...), kind=kLoop, calls=%fused_computation.29 | loop fusion | flops 27262976 | bytes 79652864 | tf_op jit(solution)/shard_map/mul | solution.py:81
  171.5 2.7 add_multiply_fusion.2
  174.2 1035.6 %while.21 = (s32[]{:T(128)}, f32[4,16,2,32,512]{4,3,2,1,0:T(8,128)}, f32[64,32,512]{2,1,0:T(8,128)}, f32[4,16]{1,0:T(4,128)S(1)}, f32[64,32,512]{2,1,0:T(8,128)}...) while((s32[]{:T(128)}, f32[4,16,2,32,512]{4,3,2,1,0:T(8,128)}, f32[64,32,512]{2,1,0:T(8,128)}, ...), condition=%wide.region_6.7_spmd, body=%wide.region_3.6_spmd.sunk | while | flops 151519248 | bytes 23069656 | solution.py:110
  186.1 254.0 %fusion.65 = (f32[16,32,512]{2,1,0:T(8,128)S(1)}, f32[16,32,512]{2,1,0:T(8,128)S(1)}) fusion(f32[64,32,512]{2,1,0:T(8,128)} %get-tuple-element.248, f32[64,32,512]{2,1,0:T(8,128)} %get-tuple-element.247, f32[16]{0:T(128)S(1)} %get-tuple-element.200, f32[64,32,512]{2,1,0:T(8,128)} %get-tuple-element.245), kind=kLoop, calls=%fused_computation.8.clone.1 | loop fusion | flops 150470656 | bytes 14680128 | tf_op jit(solution)/shard_map/while/body/eval_jaxpr/reduce_sum | solution.py:101
  440.5 1.5 copy_dynamic-update-slice_fusion.2
  442.0 254.0 %fusion.65 = (f32[16,32,512]{2,1,0:T(8,128)S(1)}, f32[16,32,512]{2,1,0:T(8,128)S(1)}) fusion(f32[64,32,512]{2,1,0:T(8,128)} %get-tuple-element.248, f32[64,32,512]{2,1,0:T(8,128)} %get-tuple-element.247, f32[16]{0:T(128)S(1)} %get-tuple-element.200, f32[64,32,512]{2,1,0:T(8,128)} %get-tuple-element.245), kind=kLoop, calls=%fused_computation.8.clone.1 | loop fusion | flops 150470656 | bytes 14680128 | tf_op jit(solution)/shard_map/while/body/eval_jaxpr/reduce_sum | solution.py:101
  696.4 1.6 copy_dynamic-update-slice_fusion.2
  697.9 254.0 %fusion.65 = (f32[16,32,512]{2,1,0:T(8,128)S(1)}, f32[16,32,512]{2,1,0:T(8,128)S(1)}) fusion(f32[64,32,512]{2,1,0:T(8,128)} %get-tuple-element.248, f32[64,32,512]{2,1,0:T(8,128)} %get-tuple-element.247, f32[16]{0:T(128)S(1)} %get-tuple-element.200, f32[64,32,512]{2,1,0:T(8,128)} %get-tuple-element.245), kind=kLoop, calls=%fused_computation.8.clone.1 | loop fusion | flops 150470656 | bytes 14680128 | tf_op jit(solution)/shard_map/while/body/eval_jaxpr/reduce_sum | solution.py:101
  952.4 1.5 copy_dynamic-update-slice_fusion.2
  953.9 254.0 %fusion.65 = (f32[16,32,512]{2,1,0:T(8,128)S(1)}, f32[16,32,512]{2,1,0:T(8,128)S(1)}) fusion(f32[64,32,512]{2,1,0:T(8,128)} %get-tuple-element.248, f32[64,32,512]{2,1,0:T(8,128)} %get-tuple-element.247, f32[16]{0:T(128)S(1)} %get-tuple-element.200, f32[64,32,512]{2,1,0:T(8,128)} %get-tuple-element.245), kind=kLoop, calls=%fused_computation.8.clone.1 | loop fusion | flops 150470656 | bytes 14680128 | tf_op jit(solution)/shard_map/while/body/eval_jaxpr/reduce_sum | solution.py:101
  1208.3 1.6 copy_dynamic-update-slice_fusion.2
  1209.9 73.9 %reduce-scatter.2.cloned.1.call-done = f32[16,2,32,512]{3,2,1,0:T(8,128)} async-done(((f32[64,2,32,512]{3,2,1,0:T(8,128)}), f32[16,2,32,512]{3,2,1,0:T(8,128)}) %reduce-scatter.2.cloned.1.call-update) | async-done | bytes 2097168 | tf_op jit(solution)/shard_map/reduce_scatter | solution.py:111
  1283.8 1.5 copy.40
  (38 shorter events, 6.1 us)
Async XLA Ops:
  7.2 1202.7 %all-reduce.10.cloned.1.call-start = ((), (), s32[]{:S(2)}) async-start(), calls=%async_computation.2 | async-start | bytes 131072 | tf_op jit(solution)/shard_map/psum | solution.py:87
  8.4 30.3 %collective-permute-start.1 = (f32[3,2,32,512]{3,2,1,0:T(8,128)S(1)}, f32[3,2,32,512]{3,2,1,0:T(8,128)S(1)}, u32[]{:S(2)}, u32[]{:S(2)}) collective-permute-start(f32[3,2,32,512]{3,2,1,0:T(8,128)S(1)} %get-tuple-element.105), channel_id=1, source_target_pairs={{0,8},{8,16},{16,24},{1,9},{9,17},{17,25},{2,10},{10,18},{18,26},{... | collective-permute-start | bytes 1179656 | tf_op jit(solution)/shard_map/ppermute | solution.py:18
  10.8 41.9 %collective-permute-start = (f32[3,2,32,512]{3,2,1,0:T(8,128)S(1)}, f32[3,2,32,512]{3,2,1,0:T(8,128)S(1)}, u32[]{:S(2)}, u32[]{:S(2)}) collective-permute-start(f32[3,2,32,512]{3,2,1,0:T(8,128)S(1)} %get-tuple-element.104), channel_id=1, source_target_pairs={{8,0},{16,8},{24,16},{9,1},{17,9},{25,17},{10,2},{18,10},{26,18},{... | collective-permute-start | bytes 1179656 | tf_op jit(solution)/shard_map/ppermute | solution.py:21
  23.8 4.8 copy-start.3
  23.8 6.1 copy-start.4
  52.7 16.4 %copy-start = (f32[64,32,512]{2,1,0:T(8,128)S(1)}, f32[64,32,512]{2,1,0:T(8,128)}, u32[]{:S(2)}) copy-start(f32[64,32,512]{2,1,0:T(8,128)} %get-tuple-element.100) | copy-start | bytes 12582916
  53.5 20.4 %copy-start.1 = (f32[3,66,32,512]{3,2,1,0:T(8,128)}, f32[3,66,32,512]{3,2,1,0:T(8,128)S(1)}, u32[]{:S(2)}) copy-start(f32[3,66,32,512]{3,2,1,0:T(8,128)S(1)} %get-tuple-element.116) | copy-start | bytes 38928388
  62.6 39.7 %collective-permute-start.2 = (f32[3,68,2,512]{3,2,1,0:T(2,128)S(1)}, f32[3,68,2,512]{3,2,1,0:T(2,128)S(1)}, u32[]{:S(2)}, u32[]{:S(2)}) collective-permute-start(f32[3,68,2,512]{3,2,1,0:T(2,128)S(1)} %get-tuple-element.97), channel_id=1, source_target_pairs={{0,1},{1,2},{2,3},{3,4},{4,5},{5,6},{6,7},{8,9},{9,10},{10,11},{11... | collective-permute-start | bytes 2506760 | tf_op jit(solution)/shard_map/ppermute | solution.py:18
  66.9 35.4 %collective-permute-start.3 = (f32[3,68,2,512]{3,2,1,0:T(2,128)S(1)}, f32[3,68,2,512]{3,2,1,0:T(2,128)S(1)}, u32[]{:S(2)}, u32[]{:S(2)}) collective-permute-start(f32[3,68,2,512]{3,2,1,0:T(2,128)S(1)} %get-tuple-element.98), channel_id=1, source_target_pairs={{1,0},{2,1},{3,2},{4,3},{5,4},{6,5},{7,6},{9,8},{10,9},{11,10},{12... | collective-permute-start | bytes 2506760 | tf_op jit(solution)/shard_map/ppermute | solution.py:21
  128.9 1.9 copy-start.2
  144.1 1139.7 %reduce-scatter.2.cloned.1.call-start = ((), (), s32[]{:S(2)}) async-start(), calls=%async_computation.1 | async-start | bytes 10485760 | tf_op jit(solution)/shard_map/reduce_scatter | solution.py:111
Sparse Core Ops, SparseCore 0:
  144.2 33.7 all-reduce.9
  1210.0 73.7 reduce-scatter.1
where the time goes:
time: 1290 us
  other arithmetic  1090 us (84%)
  waiting for transfers between devices  102 us (8%)
  local copies, waits for them, and re-layouts  58.4 us (5%)
  between operations  14.3 us (1%)
    reduce_sum x4, other arithmetic, one_block(): jnp.sum(stokes_q[None] * cosine - stokes_u[None] * sine, axis=1)  1020 us
    reduce_scatter x1, waiting for transfers between devices, body(): lax.psum_scatter(stacked.reshape(lax.axis_size('depth') * rows, 2, strip,...  73.9 us
    ppermute x2, waiting for transfers between devices, padded_2(): lax.ppermute(lax.slice_in_dim(block, block.shape[dim] - width, None, axis...  28.4 us
    mul x1, other arithmetic, body(): stokes_u = -2.0 * density * field_x * field_y  27.3 us
  transfers between devices with their start and end apart: 6, of which 2 were waited for; matrix products, arithmetic and copies ran while one was open for 85% of the time, Pallas kernels for 0%

commit v1 on v0

v1 whole, which is shorter than its diff:
```python
import functools

import jax
import jax.numpy as jnp
import numpy as np
from jax import lax
from jax.experimental import pallas as pl
from jax.experimental.pallas import tpu as pltpu
from jax.sharding import PartitionSpec as P

NCH = 64


two_pi = 6.283185307179586
faraday_coef = 0.25

REACH = 32.0
TERMS = 26


def grid_lam2():
    freq = 0.5 + 1.5 * np.arange(NCH, dtype=np.float64) / (NCH - 1)
    return 2.0 * (0.2998 / freq) ** 2


def series_table():
    lam = grid_lam2()
    middle = 0.5 * (lam.max() + lam.min())
    args = (lam - middle) * REACH
    count = 4096
    theta = (np.arange(count) + 0.5) * (np.pi / count)
    orders = np.arange(TERMS)
    table = np.cos(
        orders[None, :, None] * theta - args[:, None, None] * np.sin(theta)
    ).mean(axis=-1)
    table = table * np.where(orders == 0, 1.0, 2.0)
    table = table * np.where((orders // 2) % 2 == 0, 1.0, -1.0)
    return middle, table.astype(np.float32)


def halves_fit():
    nodes = 0.25 * (np.cos((np.arange(200) + 0.5) * np.pi / 200) + 1.0) / 2.0
    r = np.sqrt(nodes)
    root = np.sqrt(2.0)
    sin_fit = np.polynomial.polynomial.polyfit(nodes, root * np.sin(np.pi * r) / r, 4)
    cos_fit = np.polynomial.polynomial.polyfit(nodes, root * np.cos(np.pi * r), 5)
    return [float(v) for v in sin_fit], [float(v) for v in cos_fit]


SIN_FIT, COS_FIT = halves_fit()


def horner(fit, square):
    total = fit[-1] * square + fit[-2]
    for value in fit[-3::-1]:
        total = total * square + value
    return total


def turn(fraction):
    square = fraction * fraction
    sine = horner(SIN_FIT, square) * fraction
    cosine = horner(COS_FIT, square)
    return 1.0 - sine * sine, sine * cosine


def turn_of_phase(phase):
    laps = jnp.round(phase * (1.0 / two_pi))
    rest = phase - laps * 6.28125
    rest = rest - laps * 0.0019340515136718750
    rest = rest - laps * (two_pi - 6.28125 - 0.0019340515136718750)
    return turn(rest * (1.0 / two_pi))


def field_kernel(zcos, pot, zlow, zhigh, xlow, xhigh, xcos, ysin, q_out, u_out, sum_out):
    slab, strip, width = sum_out.shape
    column = lax.broadcasted_iota(jnp.int32, (strip, width), 1)
    ybase = jnp.broadcast_to(1.0 + 0.3 * ysin[...], (strip, width))
    xhalf = jnp.broadcast_to(0.5 * xcos[...], (strip, width))

    def along_last(v):
        up1 = jnp.where(column < width - 1, pltpu.roll(v, width - 1, 1), 0.0)
        up2 = jnp.where(column < width - 2, pltpu.roll(v, width - 2, 1), 0.0)
        down1 = jnp.where(column >= 1, pltpu.roll(v, 1, 1), 0.0)
        down2 = jnp.where(column >= 2, pltpu.roll(v, 2, 1), 0.0)
        return (8.0 * (up1 - down1) - (up2 - down2)) * (1.0 / 12.0)

    def along_mid(component, z):
        low = xlow[component - 1, z]
        high = xhigh[component - 1, z]
        v = jnp.concatenate([low, pot[component, z], high], axis=0)
        return (8.0 * (v[3 : strip + 3] - v[1 : strip + 1]) - (v[4 : strip + 4] - v[0:strip])) * (
            1.0 / 12.0
        )

    def along_lead(component, z, edge):
        def plane(step):
            if edge is None:
                return pot[component, z + step]
            place = edge + step
            if place < 0:
                return zlow[component, place + 2]
            if place >= slab:
                return zhigh[component, place - slab]
            return pot[component, place]

        return (8.0 * (plane(1) - plane(-1)) - (plane(2) - plane(-2))) * (1.0 / 12.0)

    def one(z, before, edge=None):
        field_x = along_last(pot[2, z]) - along_lead(1, z, edge)
        field_y = along_lead(0, z, edge) - along_mid(2, z)
        field_z = along_mid(1, z) - along_last(pot[0, z])
        density = ybase + zcos[z] * xhalf
        q_out[z] = density * (field_y * field_y - field_x * field_x)
        u_out[z] = -2.0 * density * field_x * field_y
        now = before + density * field_z
        sum_out[z] = now
        return now

    state = jnp.zeros((strip, width), jnp.float32)
    for z in (0, 1):
        state = one(z, state, z)
    state = lax.fori_loop(2, slab - 2, one, state)
    for z in (slab - 2, slab - 1):
        state = one(z, state, z)


def moment_kernel(middle, q_ref, u_ref, sum_ref, start_ref, out):
    slab, strip, width = sum_ref.shape
    group = 8 if slab % 8 == 0 else 1

    def tile(index, carry):
        row = pl.multiple_of((index // (width // 128)) * 8, 8)
        col = pl.multiple_of((index % (width // 128)) * 128, 128)
        place = (pl.ds(row, 8), pl.ds(col, 128))
        start = start_ref[place]
        for j in range(2 * TERMS):
            out[(j,) + place] = jnp.zeros((8, 128), jnp.float32)

        def block(step, carry):
            q_prev, q_now, u_prev, u_now, twice = [], [], [], [], []
            for k in range(group):
                z = step * group + k
                shift = faraday_coef * sum_ref[(z,) + place] + start
                laps = shift * (middle / two_pi)
                cosine, sine = turn(laps - jnp.round(laps))
                q = q_ref[(z,) + place]
                u = u_ref[(z,) + place]
                x = shift * (1.0 / REACH)
                q_prev.append(q * cosine - u * sine)
                u_prev.append(q * sine + u * cosine)
                twice.append(x + x)
                q_now.append(x * q_prev[-1])
                u_now.append(x * u_prev[-1])
            out[(0,) + place] += functools.reduce(jnp.add, q_prev)
            out[(TERMS,) + place] += functools.reduce(jnp.add, u_prev)
            for j in range(1, TERMS):
                out[(j,) + place] += functools.reduce(jnp.add, q_now)
                out[(TERMS + j,) + place] += functools.reduce(jnp.add, u_now)
                if j < TERMS - 1:
                    for k in range(group):
                        q_prev[k], q_now[k] = q_now[k], twice[k] * q_now[k] - q_prev[k]
                        u_prev[k], u_now[k] = u_now[k], twice[k] * u_now[k] - u_prev[k]
            return carry

        return lax.fori_loop(0, slab // group, block, carry)

    lax.fori_loop(0, (strip // 8) * (width // 128), tile, 0)


def channel_kernel(index, lam, weight, table, moments, depth_ref, out):
    rows, _, strip, width = out.shape

    def band(step, carry):
        place = pl.ds(pl.multiple_of(step * 8, 8), 8)
        half = 0.5 * depth_ref[place]

        def one(row, carry):
            base = index[row] * TERMS
            real_part = table[base] * moments[0, place]
            imag_part = table[base] * moments[TERMS, place]
            for j in range(1, TERMS):
                factor = table[base + j]
                first = factor * moments[j, place]
                second = factor * moments[TERMS + j, place]
                if j % 2 == 0:
                    real_part = real_part + first
                    imag_part = imag_part + second
                else:
                    real_part = real_part - second
                    imag_part = imag_part + first
            cosine, sine = turn_of_phase(2.0 * lam[row] * half)
            out[row, 0, place] = (real_part * cosine - imag_part * sine) * weight[row]
            out[row, 1, place] = (real_part * sine + imag_part * cosine) * weight[row]
            return carry

        return lax.fori_loop(0, rows, one, carry)

    lax.fori_loop(0, strip // 8, band, 0)


def direct_kernel(lam, weight, q_ref, u_ref, sum_ref, nearer_ref, out):
    slab, strip, width = sum_ref.shape
    twice = 2.0 * lam[pl.program_id(0)]
    scale = weight[pl.program_id(0)]

    def band(step, carry):
        place = pl.ds(pl.multiple_of(step * 8, 8), 8)
        nearer = nearer_ref[place]

        def one(z, sums):
            cosine, sine = turn_of_phase(twice * (faraday_coef * sum_ref[z, place] + nearer))
            q = q_ref[z, place]
            u = u_ref[z, place]
            return sums[0] + (q * cosine - u * sine), sums[1] + (q * sine + u * cosine)

        zero = jnp.zeros((8, width), jnp.float32)
        real_part, imag_part = lax.fori_loop(0, slab, one, (zero, zero))
        out[0, 0, place] = real_part * scale
        out[0, 1, place] = imag_part * scale
        return carry

    lax.fori_loop(0, strip // 8, band, 0)


vmem = pl.BlockSpec(memory_space=pltpu.VMEM)
smem = pl.BlockSpec(memory_space=pltpu.SMEM)
params = pltpu.CompilerParams(vmem_limit_bytes=60 * 1024 * 1024)


def neighbours(block, axis, dim):
    count = lax.axis_size(axis)
    forward = [(i, i + 1) for i in range(count - 1)]
    backward = [(target, source) for source, target in forward]
    low = lax.ppermute(
        lax.slice_in_dim(block, block.shape[dim] - 2, None, axis=dim), axis, forward
    )
    high = lax.ppermute(lax.slice_in_dim(block, 0, 2, axis=dim), axis, backward)
    return low, high


def body(potential, channel_index, patch_offsets):
    depth_count = lax.axis_size("depth")
    depth_place = lax.axis_index("depth")
    slab, strip, width = (potential.shape[1], potential.shape[2], potential.shape[3])
    zlow, zhigh = neighbours(potential[0:2], "depth", 1)
    xlow, xhigh = neighbours(potential[1:3], "tile", 2)
    zstart = depth_place * slab
    xstart = lax.axis_index("tile") * strip
    zpos = (zstart + jnp.arange(slab, dtype=jnp.int32) + patch_offsets[0]).astype(jnp.float32)
    xpos = (xstart + jnp.arange(strip, dtype=jnp.int32) + patch_offsets[1]).astype(jnp.float32)
    ypos = (jnp.arange(width, dtype=jnp.int32) + patch_offsets[2]).astype(jnp.float32)
    zcos = jnp.cos(zpos * (two_pi / 61.0))
    xcos = jnp.cos(xpos * (two_pi / 37.0))[:, None]
    ysin = jnp.sin(ypos * (two_pi / 53.0))[None, :]
    plane = jax.ShapeDtypeStruct((slab, strip, width), jnp.float32)
    stokes_q, stokes_u, slab_sums = pl.pallas_call(
        field_kernel,
        out_shape=(plane, plane, plane),
        in_specs=[smem] + [vmem] * 7,
        out_specs=(vmem, vmem, vmem),
        compiler_params=params,
    )(zcos, potential, zlow, zhigh, xlow, xhigh, xcos, ysin)

    totals = lax.all_gather(faraday_coef * slab_sums[-1], "depth")
    faraday_depth = jnp.sum(totals, axis=0)
    before = (jnp.arange(depth_count) < depth_place)[:, None, None]
    nearer = jnp.sum(jnp.where(before, totals, 0.0), axis=0)
    start = nearer - 0.5 * faraday_depth

    farthest = jnp.max(jnp.abs(faraday_coef * slab_sums + start[None]))
    farthest = lax.pmax(farthest, ("depth", "tile"))

    middle, table = series_table()
    moments = pl.pallas_call(
        functools.partial(moment_kernel, float(middle)),
        out_shape=jax.ShapeDtypeStruct((2 * TERMS, strip, width), jnp.float32),
        in_specs=[vmem] * 4,
        out_specs=vmem,
        compiler_params=params,
    )(stokes_q, stokes_u, slab_sums, start)
    moments = lax.psum(moments, "depth")

    freq = 0.5 + 1.5 * channel_index.astype(jnp.float32) / (NCH - 1)
    lam2 = (0.2998 / freq) ** 2
    weight = 1.0 / (freq * jnp.sqrt(jnp.float32(slab * depth_count)))
    rows = NCH // depth_count

    def own(values):
        return lax.dynamic_slice_in_dim(values, depth_place * rows, rows)

    def by_series(_):
        return pl.pallas_call(
            channel_kernel,
            out_shape=jax.ShapeDtypeStruct((rows, 2, strip, width), jnp.float32),
            in_specs=[smem] * 4 + [vmem] * 2,
            out_specs=vmem,
            compiler_params=params,
        )(
            own(channel_index),
            own(lam2),
            own(weight),
            jnp.asarray(table.reshape(-1)),
            moments,
            faraday_depth,
        )

    def by_sum(_):
        whole = pl.BlockSpec((slab, strip, width), lambda c: (0, 0, 0))
        sums = pl.pallas_call(
            direct_kernel,
            grid=(NCH,),
            out_shape=jax.ShapeDtypeStruct((NCH, 2, strip, width), jnp.float32),
            in_specs=[smem] * 2
            + [whole] * 3
            + [pl.BlockSpec((strip, width), lambda c: (0, 0))],
            out_specs=pl.BlockSpec((1, 2, strip, width), lambda c: (c, 0, 0, 0)),
            compiler_params=params,
        )(lam2, weight, stokes_q, stokes_u, slab_sums, nearer)
        return lax.psum_scatter(sums, "depth", scatter_dimension=0, tiled=True)

    pol_spectra = lax.cond(farthest <= REACH, by_series, by_sum, 0)
    return (pol_spectra, faraday_depth)


def solution(mesh):
    in_specs = (P(None, "depth", "tile", None), P(), P())
    out_specs = (P("depth", None, "tile", None), P("tile", None))
    return jax.shard_map(body, mesh=mesh, in_specs=in_specs, out_specs=out_specs, check_vma=False)
```

time: 1290 us -> 204 us (0.16)
  other arithmetic: 1090 us -> 8.82 us
  Pallas kernels: 0 us -> 67.5 us
  waiting for transfers between devices: 102 us -> 45.8 us
  local copies, waits for them, and re-layouts: 58.4 us -> 7.96 us
  blocking collectives: 7.48 us -> 47 us
    reduce_sum x4 -> x1, other arithmetic: 1020 us -> 0.09 us  [body(): faraday_depth = jnp.sum(totals, axis=0)]
    reduce_scatter x1 -> x0, waiting for transfers between devices: 73.9 us -> none  [body(): lax.psum_scatter(stacked.reshape(lax.axis_size('depth') * rows, 2, strip,...]
    pallas_call x0 -> x3, Pallas kernels: none -> 67.5 us  [the longest x1 33.2 us: body(): pl.pallas_call(functools.partial(moment_kernel, float(middle)), out_shape...]
    pmax x0 -> x1, blocking collectives: none -> 41.2 us  [body(): farthest = lax.pmax(farthest, ('depth', 'tile'))]
    mul x13 -> x1, other arithmetic: 33.7 us -> 0.85 us  [body(): totals = lax.all_gather(faraday_coef * slab_sums[-1], 'depth')]
    psum x1, waiting for transfers between devices: 0.02 us -> 28.7 us  [body(): moments = lax.psum(moments, 'depth')]
    slice x7 -> x3, local copies, waits for them, and re-layouts: 33.2 us -> 5.25 us  [the longest x2 3.83 us: neighbours(): high = lax.ppermute(lax.slice_in_dim(block, 0, 2, axis=dim), axis, backward)]
    unnamed x13 -> x14, local copies, waits for them, and re-layouts: 17.4 us -> 0.81 us
  transfers between devices with their start and end apart: 6 -> 5, of which waited for: 2 -> 3; matrix products, arithmetic and copies ran while one was open for 85% -> 6% of each run, Pallas kernels for 0% -> 0%
where the time goes in v1:
time: 204 us; the launch traced here: 203 us
  Pallas kernels  67.5 us (33%)
  blocking collectives  47 us (23%)
  waiting for transfers between devices  45.8 us (22%)
  between operations  14.8 us (7%)
  starting transfers between devices  11.2 us (5%)
  other arithmetic  8.82 us (4%)
  local copies, waits for them, and re-layouts  7.96 us (4%)
    pmax x1, blocking collectives, body(): farthest = lax.pmax(farthest, ('depth', 'tile'))  41.2 us
    pallas_call x1, Pallas kernels, body(): pl.pallas_call(functools.partial(moment_kernel, float(middle)), out_shape...  33.2 us
    psum x1, waiting for transfers between devices, body(): moments = lax.psum(moments, 'depth')  28.7 us
    pallas_call x1, Pallas kernels, body(): pl.pallas_call(field_kernel, out_shape=(plane, plane, plane), in_specs=[s...  24.2 us
    ppermute x2, waiting for transfers between devices, neighbours(): lax.ppermute(lax.slice_in_dim(block, block.shape[dim] - 2, None, axis=dim...  12.3 us
    pallas_call x1, Pallas kernels, by_series(): pl.pallas_call(channel_kernel, out_shape=jax.ShapeDtypeStruct((rows, 2, s...  10 us
    ppermute x2, starting transfers between devices, neighbours(): lax.ppermute(lax.slice_in_dim(block, block.shape[dim] - 2, None, axis=dim...  8.61 us
    all_gather x1, blocking collectives, body(): totals = lax.all_gather(faraday_coef * slab_sums[-1], 'depth')  5.76 us
  transfers between devices with their start and end apart: 5, of which 3 were waited for; matrix products, arithmetic and copies ran while one was open for 6% of the time, Pallas kernels for 0%

profile of v1, /device:TPU:0, one launch (start us, length us, event | category | flops | bytes accessed | tf_op | source)
XLA Modules:
  0.0 203.1 jit_solution(11806295770122725060)
XLA Ops:
  7.2 0.0 all-reduce.2.cloned.1.call-start
  7.2 1.1 fusion.2
  8.3 1.3 collective-permute-start.1
  9.6 3.0 %collective-permute-start = (f32[2,2,32,512]{3,2,1,0:T(8,128)S(1)}, f32[2,2,32,512]{3,2,1,0:T(8,128)S(1)}, u32[]{:S(2)}, u32[]{:S(2)}) collective-permute-start(f32[2,2,32,512]{3,2,1,0:T(8,128)S(1)} %get-tuple-element.57), channel_id=1, source_target_pairs={{0,8},{8,16},{16,24},{1,9},{9,17},{17,25},{2,10},{10,18},{18,26},{... | collective-permute-start | bytes 786440 | tf_op jit(solution)/shard_map/ppermute | solution.py:235
  12.6 2.8 %fusion.1 = (f32[2,64,2,512]{3,2,1,0:T(2,128)S(1)}, f32[2,64,2,512]{3,2,1,0:T(2,128)S(1)}) fusion(f32[3,64,32,512]{3,2,1,0:T(8,128)} %pot.1), kind=kLoop, calls=%fused_computation.12 | loop fusion | bytes 2097152 | tf_op jit(solution)/shard_map/slice | solution.py:238
  15.4 1.3 collective-permute-start.3
  16.7 5.6 %collective-permute-start.2 = (f32[2,64,2,512]{3,2,1,0:T(2,128)S(1)}, f32[2,64,2,512]{3,2,1,0:T(2,128)S(1)}, u32[]{:S(2)}, u32[]{:S(2)}) collective-permute-start(f32[2,64,2,512]{3,2,1,0:T(2,128)S(1)} %get-tuple-element.55), channel_id=1, source_target_pairs={{0,1},{1,2},{2,3},{3,4},{4,5},{5,6},{6,7},{8,9},{9,10},{10,11},{11... | collective-permute-start | bytes 1572872 | tf_op jit(solution)/shard_map/ppermute | solution.py:235
  22.3 1.4 fusion.3
  23.7 1.3 multiply_cosine_fusion.1.zcos
  25.0 1.3 multiply_sine_fusion.ysin
  26.3 1.4 multiply_cosine_fusion.xcos
  27.6 0.0 collective-permute-done.1.zhigh
  27.6 0.0 collective-permute-done.zlow
  27.7 4.8 %collective-permute-done.3.xhigh = f32[2,64,2,512]{3,2,1,0:T(2,128)S(1)} collective-permute-done((f32[2,64,2,512]{3,2,1,0:T(2,128)S(1)}, f32[2,64,2,512]{3,2,1,0:T(2,128)S(1)}, u32[]{:S(2)}, u32[]{:S(2)}) %collective-permute-start.3) | collective-permute-done | bytes 524320 | tf_op jit(solution)/shard_map/ppermute | solution.py:238
  32.5 12.3 %collective-permute-done.2.xlow = f32[2,64,2,512]{3,2,1,0:T(2,128)S(1)} collective-permute-done((f32[2,64,2,512]{3,2,1,0:T(2,128)S(1)}, f32[2,64,2,512]{3,2,1,0:T(2,128)S(1)}, u32[]{:S(2)}, u32[]{:S(2)}) %collective-permute-start.2) | collective-permute-done | bytes 524320 | tf_op jit(solution)/shard_map/ppermute | solution.py:235
  44.7 0.8 copy-done.3
  45.5 24.2 %shard_map.60 = (f32[64,32,512]{2,1,0:T(8,128)}, f32[64,32,512]{2,1,0:T(8,128)}, f32[64,32,512]{2,1,0:T(8,128)}) custom-call(f32[64]{0:T(128)} %multiply_cosine_fusion.1.zcos, f32[3,64,32,512]{3,2,1,0:T(8,128)} %pot.1, f32[2,2,32,512]{3,2,1,0:T(8,128)} %copy-done.5, f32[2,2,32,512]{3,2,1,0:T(8,128)} %copy-done.4, f32[2,64,2,512]{3,2,1,0:T(2,128)} %copy-done.3, ...), custom_call_target="tpu_custom_call" | custom-call | tf_op jit(solution)/shard_map/pallas_call | solution.py:257
  69.7 0.8 slice_multiply_fusion
  70.6 5.8 %all_gather.4 = f32[4,32,512]{2,1,0:T(8,128)S(1)} all-gather(f32[1,32,512]{2,1,0:T(8,128)S(1)} %slice_multiply_fusion), channel_id=1, replica_groups=mesh['depth'=4,'tile'=8] {'depth'}, dimensions={0}, use_global_device_ids=true | all-gather | bytes 327680 | tf_op jit(solution)/shard_map/all_gather | solution.py:265
  76.4 0.1 fusion
  76.4 0.0 copy-start.1
  76.5 0.7 multiply_subtract_fusion.start_ref
  77.1 33.2 %shard_map.61 = f32[52,32,512]{2,1,0:T(8,128)} custom-call(f32[64,32,512]{2,1,0:T(8,128)} %get-tuple-element.48.q_ref, f32[64,32,512]{2,1,0:T(8,128)} %get-tuple-element.49.u_ref, f32[64,32,512]{2,1,0:T(8,128)} %get-tuple-element.47.sum_ref, f32[32,512]{1,0:T(8,128)} %multiply_subtract_fusion.start_ref), custom_call_target="tpu_custom_call" | custom-call | tf_op jit(solution)/shard_map/pallas_call | solution.py:275
  110.3 0.0 all-reduce.2.cloned.1.call-update
  110.4 3.3 %abs_reduce_fusion = f32[]{:T(128)} fusion(f32[64,32,512]{2,1,0:T(8,128)} %get-tuple-element.47.sum_ref, f32[32,512]{1,0:T(8,128)S(1)} %copy-done), kind=kLoop, calls=%fused_computation | loop fusion | flops 4194303 | bytes 4259844 | tf_op jit(solution)/shard_map/reduce_max | solution.py:271
  113.7 41.2 %pmax.7 = f32[]{:T(128)} all-reduce(f32[]{:T(128)} %abs_reduce_fusion), channel_id=1, replica_groups=mesh['depth'=4,'tile'=8] {'depth','tile'}, use_global_device_ids=true, to_apply=%region_3.4 | all-reduce | flops 1 | bytes 8 | tf_op jit(solution)/shard_map/pmax | solution.py:272
  155.6 28.7 %all-reduce.2.cloned.1.call-done = f32[52,32,512]{2,1,0:T(8,128)} async-done(((f32[52,32,512]{2,1,0:T(8,128)}), f32[52,32,512]{2,1,0:T(8,128)}) %all-reduce.2.cloned.1.call-update) | async-done | bytes 3407888 | tf_op jit(solution)/shard_map/psum | solution.py:282
  184.3 11.9 %conditional.1 = (f32[16,2,32,512]{3,2,1,0:T(8,128)}) conditional(s32[]{:T(128)} %convert_element_type.32, (f32[64]{0:T(128)S(1)}, f32[64]{0:T(128)S(1)}, f32[64,32,512]{2,1,0:T(8,128)}, f32[64,32,512]{2,1,0:T(8,128)}, f32[64,32,512]{2,1,0:T(8,128)}, /*index=5*/f32[32,512]{1,0:T(8,128)S(1)}) %tuple.14, (s32[]{:T(128)}, s32[64]{0:T(128)S(1)}, ...), branch_computations={%region_5.7_spmd, %region_7.8_spmd} | conditional | flops 4 | bytes 31457328 | solution.py:322
  184.3 0.7 dynamic_slice.6.index
  185.0 0.6 dynamic_slice.7.lam
  185.6 0.6 dynamic_slice.8.weight
  186.2 10.0 %branch_1_fun.1 = f32[16,2,32,512]{3,2,1,0:T(8,128)} custom-call(s32[16]{0:T(128)} %dynamic_slice.6.index, f32[16]{0:T(128)} %dynamic_slice.7.lam, f32[16]{0:T(128)} %dynamic_slice.8.weight, f32[1664]{0:T(1024)} %constant.49.clone.1.table, f32[52,32,512]{2,1,0:T(8,128)} %get-tuple-element.40.moments, f32[32,512]{1,0:T(8,128)S(1)} %get-tuple-element.41.depth_ref), custom_call_target="tpu_custom_call" | custom-call | tf_op jit(solution)/shard_map/cond/branch_1_fun/pallas_call | solution.py:293
  (14 shorter events, 0.0 us)
Async XLA Ops:
  7.2 177.1 %all-reduce.2.cloned.1.call-start = ((), (), s32[]{:S(2)}) async-start(), calls=%async_computation.2 | async-start | bytes 6815744 | tf_op jit(solution)/shard_map/psum | solution.py:282
  8.3 19.3 %collective-permute-start.1 = (f32[2,2,32,512]{3,2,1,0:T(8,128)S(1)}, f32[2,2,32,512]{3,2,1,0:T(8,128)S(1)}, u32[]{:S(2)}, u32[]{:S(2)}) collective-permute-start(f32[2,2,32,512]{3,2,1,0:T(8,128)S(1)} %get-tuple-element.56), channel_id=1, source_target_pairs={{8,0},{16,8},{24,16},{9,1},{17,9},{25,17},{10,2},{18,10},{26,18},{... | collective-permute-start | bytes 786440 | tf_op jit(solution)/shard_map/ppermute | solution.py:238
  9.6 18.0 %collective-permute-start = (f32[2,2,32,512]{3,2,1,0:T(8,128)S(1)}, f32[2,2,32,512]{3,2,1,0:T(8,128)S(1)}, u32[]{:S(2)}, u32[]{:S(2)}) collective-permute-start(f32[2,2,32,512]{3,2,1,0:T(8,128)S(1)} %get-tuple-element.57), channel_id=1, source_target_pairs={{0,8},{8,16},{16,24},{1,9},{9,17},{17,25},{2,10},{10,18},{18,26},{... | collective-permute-start | bytes 786440 | tf_op jit(solution)/shard_map/ppermute | solution.py:235
  15.4 17.0 %collective-permute-start.3 = (f32[2,64,2,512]{3,2,1,0:T(2,128)S(1)}, f32[2,64,2,512]{3,2,1,0:T(2,128)S(1)}, u32[]{:S(2)}, u32[]{:S(2)}) collective-permute-start(f32[2,64,2,512]{3,2,1,0:T(2,128)S(1)} %get-tuple-element.54), channel_id=1, source_target_pairs={{1,0},{2,1},{3,2},{4,3},{5,4},{6,5},{7,6},{9,8},{10,9},{11,10},{12... | collective-permute-start | bytes 1572872 | tf_op jit(solution)/shard_map/ppermute | solution.py:238
  16.7 28.0 %collective-permute-start.2 = (f32[2,64,2,512]{3,2,1,0:T(2,128)S(1)}, f32[2,64,2,512]{3,2,1,0:T(2,128)S(1)}, u32[]{:S(2)}, u32[]{:S(2)}) collective-permute-start(f32[2,64,2,512]{3,2,1,0:T(2,128)S(1)} %get-tuple-element.55), channel_id=1, source_target_pairs={{0,1},{1,2},{2,3},{3,4},{4,5},{5,6},{6,7},{8,9},{9,10},{10,11},{11... | collective-permute-start | bytes 1572872 | tf_op jit(solution)/shard_map/ppermute | solution.py:235
  27.6 17.1 %copy-start.4 = (f32[2,2,32,512]{3,2,1,0:T(8,128)}, f32[2,2,32,512]{3,2,1,0:T(8,128)S(1)}, u32[]{:S(2)}) copy-start(f32[2,2,32,512]{3,2,1,0:T(8,128)S(1)} %collective-permute-done.1.zhigh) | copy-start | bytes 786436
  27.6 17.1 %copy-start.5 = (f32[2,2,32,512]{3,2,1,0:T(8,128)}, f32[2,2,32,512]{3,2,1,0:T(8,128)S(1)}, u32[]{:S(2)}) copy-start(f32[2,2,32,512]{3,2,1,0:T(8,128)S(1)} %collective-permute-done.zlow) | copy-start | bytes 786436
  32.5 12.3 %copy-start.2 = (f32[2,64,2,512]{3,2,1,0:T(2,128)}, f32[2,64,2,512]{3,2,1,0:T(2,128)S(1)}, u32[]{:S(2)}) copy-start(f32[2,64,2,512]{3,2,1,0:T(2,128)S(1)} %collective-permute-done.3.xhigh) | copy-start | bytes 1572868
  44.7 0.8 copy-start.3
  76.4 107.9 %copy-start.1 = (f32[32,512]{1,0:T(8,128)}, f32[32,512]{1,0:T(8,128)S(1)}, u32[]{:S(2)}) copy-start(f32[32,512]{1,0:T(8,128)S(1)} %get-tuple-element.52) | copy-start | bytes 196612
  77.1 33.2 %copy-start.6 = (s32[64]{0:T(128)S(1)}, s32[64]{0:T(128)}, u32[]{:S(2)}) copy-start(s32[64]{0:T(128)} %param.7) | copy-start | bytes 772
  77.1 33.3 %copy-start = (f32[32,512]{1,0:T(8,128)S(1)}, f32[32,512]{1,0:T(8,128)}, u32[]{:S(2)}) copy-start(f32[32,512]{1,0:T(8,128)} %multiply_subtract_fusion.start_ref) | copy-start | bytes 196612
Sparse Core Ops, SparseCore 0:
  110.5 73.7 all-reduce.1

commit v2 on v1

--- a/solution.py
+++ b/solution.py
@@ -14,8 +14,8 @@
 two_pi = 6.283185307179586
 faraday_coef = 0.25
 
-REACH = 32.0
-TERMS = 26
+REACH = 24.0
+TERMS = 22
 
 
 def grid_lam2():
@@ -72,7 +72,7 @@
     return turn(rest * (1.0 / two_pi))
 
 
-def field_kernel(zcos, pot, zlow, zhigh, xlow, xhigh, xcos, ysin, q_out, u_out, sum_out):
+def field_kernel(zcos, pot, zlow, zhigh, xlow, xhigh, xcos, ysin, q_out, u_out, sum_out, total_out, high_out, low_out):
     slab, strip, width = sum_out.shape
     column = lax.broadcasted_iota(jnp.int32, (strip, width), 1)
     ybase = jnp.broadcast_to(1.0 + 0.3 * ysin[...], (strip, width))
@@ -106,7 +106,8 @@
 
         return (8.0 * (plane(1) - plane(-1)) - (plane(2) - plane(-2))) * (1.0 / 12.0)
 
-    def one(z, before, edge=None):
+    def one(z, state, edge=None):
+        before, high, low = state
         field_x = along_last(pot[2, z]) - along_lead(1, z, edge)
         field_y = along_lead(0, z, edge) - along_mid(2, z)
         field_z = along_mid(1, z) - along_last(pot[0, z])
@@ -115,27 +116,158 @@
         u_out[z] = -2.0 * density * field_x * field_y
         now = before + density * field_z
         sum_out[z] = now
-        return now
-
-    state = jnp.zeros((strip, width), jnp.float32)
+        return now, jnp.maximum(high, now), jnp.minimum(low, now)
+
+    zero = jnp.zeros((strip, width), jnp.float32)
+    state = (zero, zero, zero)
     for z in (0, 1):
         state = one(z, state, z)
     state = lax.fori_loop(2, slab - 2, one, state)
     for z in (slab - 2, slab - 1):
         state = one(z, state, z)
-
-
-def moment_kernel(middle, q_ref, u_ref, sum_ref, start_ref, out):
+    total_out[...] = faraday_coef * state[0]
+    high_out[...] = faraday_coef * state[1]
+    low_out[...] = faraday_coef * state[2]
+
+
+def halo_kernel(zup, zdown, xup, xdown, zlow, zhigh, xlow, xhigh, send, recv):
+    barrier = pltpu.get_barrier_semaphore()
+    plan = []
+    for order, (axis, up, down, low, high) in enumerate(
+        (("depth", zup, zdown, zlow, zhigh), ("tile", xup, xdown, xlow, xhigh))
+    ):
+        place = lax.axis_index(axis)
+        last = lax.axis_size(axis) - 1
+        above = pltpu.make_async_remote_copy(
+            src_ref=up, dst_ref=low, send_sem=send.at[2 * order], recv_sem=recv.at[2 * order],
+            device_id={axis: place + 1}, device_id_type=pl.DeviceIdType.MESH,
+        )
+        below = pltpu.make_async_remote_copy(
+            src_ref=down, dst_ref=high, send_sem=send.at[2 * order + 1],
+            recv_sem=recv.at[2 * order + 1],
+            device_id={axis: place - 1}, device_id_type=pl.DeviceIdType.MESH,
+        )
+        plan.append((axis, place, last, above, below, low, high))
+
+    def signal(axis, index):
+        pl.semaphore_signal(
+            barrier, inc=1, device_id={axis: index}, device_id_type=pl.DeviceIdType.MESH
+        )
+
+    for axis, place, last, above, below, low, high in plan:
+        pl.when(place > 0)(functools.partial(signal, axis, place - 1))
+        pl.when(place < last)(functools.partial(signal, axis, place + 1))
+    count = 0
+    for axis, place, last, above, below, low, high in plan:
+        count = count + (place + last - 1) // last + (2 * last - place - 1) // last
+    pl.semaphore_wait(barrier, count)
+    for axis, place, last, above, below, low, high in reversed(plan):
+        pl.when(place < last)(above.start)
+        pl.when(place > 0)(below.start)
+    for axis, place, last, above, below, low, high in plan:
+
+        @pl.when(place == 0)
+        def _():
+            low[...] = jnp.zeros_like(low)
+
+        @pl.when(place == last)
+        def _():
+            high[...] = jnp.zeros_like(high)
+
+    for axis, place, last, above, below, low, high in plan:
+
+        @pl.when(place < last)
+        def _():
+            above.wait_send()
+            below.wait_recv()
+
+        @pl.when(place > 0)
+        def _():
+            below.wait_send()
+            above.wait_recv()
+
+
+def moment_kernel(
+    middle, q_ref, u_ref, sum_ref, total_ref, high_ref, low_ref,
+    out, depth_out, far_out,
+    others, start_ref, own, near, part, across, far, far_depth, far_mid, far_tile,
+    carry_send, carry_recv, far_send, far_recv, tile_send, tile_recv,
+    near_send, near_recv, cross_send, cross_recv, back_send, back_recv,
+):
     slab, strip, width = sum_ref.shape
     group = 8 if slab % 8 == 0 else 1
-
-    def tile(index, carry):
-        row = pl.multiple_of((index // (width // 128)) * 8, 8)
-        col = pl.multiple_of((index % (width // 128)) * 128, 128)
-        place = (pl.ds(row, 8), pl.ds(col, 128))
+    chunks = strip // 8
+    depth_count, tile_count = lax.axis_size("depth"), lax.axis_size("tile")
+    depth_place, tile_place = lax.axis_index("depth"), lax.axis_index("tile")
+    core = lax.rem(depth_place, 2)
+    chip_count = depth_count // 2
+    chip = depth_place // 2
+    partner = depth_place + 1 - 2 * core
+
+    def copy(src, dst, send, recv, axis, index):
+        return pltpu.make_async_remote_copy(
+            src_ref=src, dst_ref=dst, send_sem=send, recv_sem=recv,
+            device_id={axis: index}, device_id_type=pl.DeviceIdType.MESH,
+        )
+
+    def depth_peer(k):
+        return lax.rem(depth_place + k, depth_count)
+
+    def tile_peer(k):
+        return lax.rem(tile_place + k, tile_count)
+
+    barrier = pltpu.get_barrier_semaphore()
+    for k in range(1, depth_count):
+        pl.semaphore_signal(
+            barrier, inc=1, device_id={"depth": depth_peer(k)},
+            device_id_type=pl.DeviceIdType.MESH,
+        )
+    for k in range(1, tile_count):
+        pl.semaphore_signal(
+            barrier, inc=1, device_id={"tile": tile_peer(k)},
+            device_id_type=pl.DeviceIdType.MESH,
+        )
+    pl.semaphore_wait(barrier, depth_count + tile_count - 2)
+
+    carries = [
+        copy(total_ref, others.at[k - 1], carry_send.at[k - 1], carry_recv.at[k - 1],
+             "depth", depth_peer(k))
+        for k in range(1, depth_count)
+    ]
+    for item in carries:
+        item.start()
+    for item in carries:
+        item.wait()
+    nearer = jnp.zeros((strip, width), jnp.float32)
+    whole = total_ref[...]
+    for k in range(1, depth_count):
+        part_k = others[k - 1]
+        whole = whole + part_k
+        nearer = nearer + jnp.where(depth_place >= k, part_k, 0.0)
+    depth_out[...] = whole
+    start = nearer - 0.5 * whole
+    start_ref[...] = start
+    reach = jnp.maximum(jnp.abs(high_ref[...] + start), jnp.abs(low_ref[...] + start))
+    reach = functools.reduce(
+        jnp.maximum, [reach[:, k * 128 : (k + 1) * 128] for k in range(width // 128)]
+    )
+    far[...] = functools.reduce(jnp.maximum, [reach[k * 8 : k * 8 + 8] for k in range(chunks)])
+    fars = [
+        copy(far, far_depth.at[k - 1], far_send.at[k - 1], far_recv.at[k - 1],
+             "depth", depth_peer(k))
+        for k in range(1, depth_count)
+    ]
+    for item in fars:
+        item.start()
+
+    def tile(row, col, g):
+        rows = pl.ds(pl.multiple_of(row, 8), 8)
+        cols = pl.ds(pl.multiple_of(col, 128), 128)
+        place = (rows, cols)
         start = start_ref[place]
-        for j in range(2 * TERMS):
-            out[(j,) + place] = jnp.zeros((8, 128), jnp.float32)
+        for half in range(2):
+            for j in range(TERMS):
+                own[g, half, j, :, cols] = jnp.zeros((8, 128), jnp.float32)
 
         def block(step, carry):
             q_prev, q_now, u_prev, u_now, twice = [], [], [], [], []
@@ -152,20 +284,85 @@
                 twice.append(x + x)
                 q_now.append(x * q_prev[-1])
                 u_now.append(x * u_prev[-1])
-            out[(0,) + place] += functools.reduce(jnp.add, q_prev)
-            out[(TERMS,) + place] += functools.reduce(jnp.add, u_prev)
+            own[g, 0, 0, :, cols] += functools.reduce(jnp.add, q_prev)
+            own[g, 1, 0, :, cols] += functools.reduce(jnp.add, u_prev)
             for j in range(1, TERMS):
-                out[(j,) + place] += functools.reduce(jnp.add, q_now)
-                out[(TERMS + j,) + place] += functools.reduce(jnp.add, u_now)
+                own[g, 0, j, :, cols] += functools.reduce(jnp.add, q_now)
+                own[g, 1, j, :, cols] += functools.reduce(jnp.add, u_now)
                 if j < TERMS - 1:
                     for k in range(group):
                         q_prev[k], q_now[k] = q_now[k], twice[k] * q_now[k] - q_prev[k]
                         u_prev[k], u_now[k] = u_now[k], twice[k] * u_now[k] - u_prev[k]
             return carry
 
-        return lax.fori_loop(0, slab // group, block, carry)
-
-    lax.fori_loop(0, (strip // 8) * (width // 128), tile, 0)
+        lax.fori_loop(0, slab // group, block, 0)
+
+    def near_copy(g):
+        return copy(own.at[g, 1 - core], near.at[g], near_send.at[g], near_recv.at[g],
+                    "depth", partner)
+
+    def cross_copies(g):
+        return [
+            copy(part.at[g], across.at[g, k - 1], cross_send.at[g, k - 1],
+                 cross_recv.at[g, k - 1], "depth", 2 * lax.rem(chip + k, chip_count) + core)
+            for k in range(1, chip_count)
+        ]
+
+    def back_copy(g):
+        piece = out.at[core, :, pl.ds(pl.multiple_of(g * 8, 8), 8)]
+        return copy(piece, piece, back_send.at[g], back_recv.at[g], "depth", partner)
+
+    def compute(g):
+        lax.fori_loop(
+            0, width // 128, lambda c, carry: (tile(g * 8, c * 128, g), carry)[1], 0
+        )
+        near_copy(g).start()
+
+    def sum_chip(g):
+        near_copy(g).wait()
+        part[g] = own[g, core] + near[g]
+        for item in cross_copies(g):
+            item.start()
+
+    def sum_all(g):
+        total = part[g]
+        for k, item in enumerate(cross_copies(g)):
+            item.wait()
+            total = total + across[g, k]
+        out[core, :, pl.ds(pl.multiple_of(g * 8, 8), 8)] = total
+        back_copy(g).start()
+
+    tiles_far = [
+        copy(far_mid, far_tile.at[k - 1], tile_send.at[k - 1], tile_recv.at[k - 1],
+             "tile", tile_peer(k))
+        for k in range(1, tile_count)
+    ]
+
+    def lap(g, carry):
+        pl.when(g < chunks)(lambda: compute(g))
+
+        @pl.when(g == 0)
+        def _():
+            reach = far[...]
+            for k, item in enumerate(fars):
+                item.wait()
+                reach = jnp.maximum(reach, far_depth[k])
+            far_mid[...] = reach
+            for item in tiles_far:
+                item.start()
+
+        pl.when(jnp.logical_and(g >= 1, g <= chunks))(lambda: sum_chip(g - 1))
+        pl.when(g >= 2)(lambda: sum_all(g - 2))
+        return carry
+
+    lax.fori_loop(0, chunks + 2, lap, 0)
+    reach = far_mid[...]
+    for k, item in enumerate(tiles_far):
+        item.wait()
+        reach = jnp.maximum(reach, far_tile[k])
+    far_out[...] = reach
+    for g in range(chunks):
+        back_copy(g).wait()
 
 
 def channel_kernel(index, lam, weight, table, moments, depth_ref, out):
@@ -177,12 +374,12 @@
 
         def one(row, carry):
             base = index[row] * TERMS
-            real_part = table[base] * moments[0, place]
-            imag_part = table[base] * moments[TERMS, place]
+            real_part = table[base] * moments[0, 0, place]
+            imag_part = table[base] * moments[1, 0, place]
             for j in range(1, TERMS):
                 factor = table[base + j]
-                first = factor * moments[j, place]
-                second = factor * moments[TERMS + j, place]
+                first = factor * moments[0, j, place]
+                second = factor * moments[1, j, place]
                 if j % 2 == 0:
                     real_part = real_part + first
                     imag_part = imag_part + second
@@ -228,23 +425,24 @@
 params = pltpu.CompilerParams(vmem_limit_bytes=60 * 1024 * 1024)
 
 
-def neighbours(block, axis, dim):
-    count = lax.axis_size(axis)
-    forward = [(i, i + 1) for i in range(count - 1)]
-    backward = [(target, source) for source, target in forward]
-    low = lax.ppermute(
-        lax.slice_in_dim(block, block.shape[dim] - 2, None, axis=dim), axis, forward
-    )
-    high = lax.ppermute(lax.slice_in_dim(block, 0, 2, axis=dim), axis, backward)
-    return low, high
-
-
 def body(potential, channel_index, patch_offsets):
     depth_count = lax.axis_size("depth")
     depth_place = lax.axis_index("depth")
     slab, strip, width = (potential.shape[1], potential.shape[2], potential.shape[3])
-    zlow, zhigh = neighbours(potential[0:2], "depth", 1)
-    xlow, xhigh = neighbours(potential[1:3], "tile", 2)
+    shapes = [(2, 2, strip, width)] * 2 + [(2, slab, 2, width)] * 2
+    zlow, zhigh, xlow, xhigh = pl.pallas_call(
+        halo_kernel,
+        out_shape=tuple(jax.ShapeDtypeStruct(shape, jnp.float32) for shape in shapes),
+        in_specs=[vmem] * 4,
+        out_specs=(vmem,) * 4,
+        scratch_shapes=[pltpu.SemaphoreType.DMA((4,)), pltpu.SemaphoreType.DMA((4,))],
+        compiler_params=pltpu.CompilerParams(collective_id=0, has_side_effects=True),
+    )(
+        potential[0:2, slab - 2 :],
+        potential[0:2, :2],
+        potential[1:3, :, strip - 2 :],
+        potential[1:3, :, :2],
+    )
     zstart = depth_place * slab
     xstart = lax.axis_index("tile") * strip
     zpos = (zstart + jnp.arange(slab, dtype=jnp.int32) + patch_offsets[0]).astype(jnp.float32)
@@ -254,32 +452,52 @@
     xcos = jnp.cos(xpos * (two_pi / 37.0))[:, None]
     ysin = jnp.sin(ypos * (two_pi / 53.0))[None, :]
     plane = jax.ShapeDtypeStruct((slab, strip, width), jnp.float32)
-    stokes_q, stokes_u, slab_sums = pl.pallas_call(
+    flat = jax.ShapeDtypeStruct((strip, width), jnp.float32)
+    stokes_q, stokes_u, slab_sums, own_total, highest, lowest = pl.pallas_call(
         field_kernel,
-        out_shape=(plane, plane, plane),
+        out_shape=(plane, plane, plane, flat, flat, flat),
         in_specs=[smem] + [vmem] * 7,
-        out_specs=(vmem, vmem, vmem),
+        out_specs=(vmem,) * 6,
         compiler_params=params,
     )(zcos, potential, zlow, zhigh, xlow, xhigh, xcos, ysin)
 
-    totals = lax.all_gather(faraday_coef * slab_sums[-1], "depth")
-    faraday_depth = jnp.sum(totals, axis=0)
-    before = (jnp.arange(depth_count) < depth_place)[:, None, None]
-    nearer = jnp.sum(jnp.where(before, totals, 0.0), axis=0)
-    start = nearer - 0.5 * faraday_depth
-
-    farthest = jnp.max(jnp.abs(faraday_coef * slab_sums + start[None]))
-    farthest = lax.pmax(farthest, ("depth", "tile"))
-
     middle, table = series_table()
-    moments = pl.pallas_call(
+    tile_count = lax.axis_size("tile")
+    chunks, chip_count = strip // 8, depth_count // 2
+    half = (TERMS, 8, width)
+    small = (8, 128)
+    dma = pltpu.SemaphoreType.DMA
+    pair = [dma((depth_count - 1,))] * 4 + [dma((tile_count - 1,))] * 2
+    moments, faraday_depth, farthest = pl.pallas_call(
         functools.partial(moment_kernel, float(middle)),
-        out_shape=jax.ShapeDtypeStruct((2 * TERMS, strip, width), jnp.float32),
-        in_specs=[vmem] * 4,
-        out_specs=vmem,
-        compiler_params=params,
-    )(stokes_q, stokes_u, slab_sums, start)
-    moments = lax.psum(moments, "depth")
+        out_shape=(
+            jax.ShapeDtypeStruct((2, TERMS, strip, width), jnp.float32),
+            flat,
+            jax.ShapeDtypeStruct(small, jnp.float32),
+        ),
+        in_specs=[vmem] * 6,
+        out_specs=(vmem,) * 3,
+        scratch_shapes=[
+            pltpu.VMEM((depth_count - 1, strip, width), jnp.float32),
+            pltpu.VMEM((strip, width), jnp.float32),
+            pltpu.VMEM((chunks, 2) + half, jnp.float32),
+            pltpu.VMEM((chunks,) + half, jnp.float32),
+            pltpu.VMEM((chunks,) + half, jnp.float32),
+            pltpu.VMEM((chunks, chip_count - 1) + half, jnp.float32),
+            pltpu.VMEM(small, jnp.float32),
+            pltpu.VMEM((depth_count - 1,) + small, jnp.float32),
+            pltpu.VMEM(small, jnp.float32),
+            pltpu.VMEM((tile_count - 1,) + small, jnp.float32),
+        ]
+        + pair
+        + [dma((chunks,))] * 2
+        + [dma((chunks, chip_count - 1))] * 2
+        + [dma((chunks,))] * 2,
+        compiler_params=pltpu.CompilerParams(
+            collective_id=1, has_side_effects=True, vmem_limit_bytes=60 * 1024 * 1024
+        ),
+    )(stokes_q, stokes_u, slab_sums, own_total, highest, lowest)
+    farthest = jnp.max(farthest)
 
     freq = 0.5 + 1.5 * channel_index.astype(jnp.float32) / (NCH - 1)
     lam2 = (0.2998 / freq) ** 2
@@ -306,6 +524,9 @@
         )
 
     def by_sum(_):
+        totals = lax.all_gather(own_total, "depth")
+        before = (jnp.arange(depth_count) < depth_place)[:, None, None]
+        nearer = jnp.sum(jnp.where(before, totals, 0.0), axis=0)
         whole = pl.BlockSpec((slab, strip, width), lambda c: (0, 0, 0))
         sums = pl.pallas_call(
             direct_kernel,

time: 204 us -> 153 us (0.75)
  Pallas kernels: 67.5 us -> 123 us
  blocking collectives: 47 us -> 0 us
  waiting for transfers between devices: 45.8 us -> 0 us
  starting transfers between devices: 11.2 us -> 0 us
  other arithmetic: 8.82 us -> 5.78 us
    pmax x1 -> x0, blocking collectives: 41.2 us -> none  [body(): farthest = lax.pmax(farthest, ('depth', 'tile'))]
    pallas_call x1 -> x2, Pallas kernels: 24.2 us -> 54.3 us  [the longest x1 28.5 us: body(): pl.pallas_call(halo_kernel, out_shape=tuple((jax.ShapeDtypeStruct(shape,...]
    psum x1 -> x0, waiting for transfers between devices: 28.7 us -> none  [body(): moments = lax.psum(moments, 'depth')]
    pallas_call x1, Pallas kernels: 33.2 us -> 61 us  [body(): pl.pallas_call(functools.partial(moment_kernel, float(middle)), out_shape...]
    ppermute x4 -> x0, waiting for transfers between devices: 17.1 us -> none  [the longest x2 12.3 us: neighbours(): lax.ppermute(lax.slice_in_dim(block, block.shape[dim] - 2, None, axis=dim...]
    ppermute x4 -> x0, starting transfers between devices: 11.2 us -> none  [the longest x2 8.61 us: neighbours(): lax.ppermute(lax.slice_in_dim(block, block.shape[dim] - 2, None, axis=dim...]
    all_gather x1 -> x0, blocking collectives: 5.76 us -> none  [body(): totals = lax.all_gather(faraday_coef * slab_sums[-1], 'depth')]
    pallas_call x1, Pallas kernels: 10 us -> 8 us  [by_series(): pl.pallas_call(channel_kernel, out_shape=jax.ShapeDtypeStruct((rows, 2, s...]
  transfers between devices with their start and end apart: 5 -> 0, of which waited for: 3 -> 0; matrix products, arithmetic and copies ran while one was open for 6% -> 0% of each run, Pallas kernels for 0% -> 0%
where the time goes in v2:
time: 153 us
  Pallas kernels  123 us (80%)
  between operations  14.7 us (10%)
  local copies, waits for them, and re-layouts  9.39 us (6%)
  other arithmetic  5.78 us (4%)
    pallas_call x1, Pallas kernels, body(): pl.pallas_call(functools.partial(moment_kernel, float(middle)), out_shape...  61 us
    pallas_call x1, Pallas kernels, body(): pl.pallas_call(halo_kernel, out_shape=tuple((jax.ShapeDtypeStruct(shape,...  28.5 us
    pallas_call x1, Pallas kernels, body(): pl.pallas_call(field_kernel, out_shape=(plane, plane, plane, flat, flat,...  25.7 us
    pallas_call x1, Pallas kernels, by_series(): pl.pallas_call(channel_kernel, out_shape=jax.ShapeDtypeStruct((rows, 2, s...  8 us
    slice x1, local copies, waits for them, and re-layouts, body(): potential[1:3, :, :2]  3.72 us

profile of v2, /device:TPU:0, one launch (start us, length us, event | category | flops | bytes accessed | tf_op | source)
XLA Modules:
  0.0 153.2 jit_solution(15071004824423359475)
XLA Ops:
  7.2 0.7 multiply_divide_fusion
  7.8 1.4 fusion.2
  9.2 1.3 multiply_cosine_fusion.1.zcos
  10.5 1.3 multiply_sine_fusion.ysin
  11.8 1.2 multiply_cosine_fusion.xcos
  13.0 1.9 %fusion.1 = (f32[2,2,32,512]{3,2,1,0:T(8,128)}, f32[2,2,32,512]{3,2,1,0:T(8,128)}) fusion(f32[3,64,32,512]{3,2,1,0:T(8,128)} %pot.1), kind=kLoop, calls=%fused_computation.9 | loop fusion | bytes 1048576 | tf_op jit(solution)/shard_map/slice | solution.py:442
  14.9 3.7 %fusion = (f32[2,64,2,512]{3,2,1,0:T(2,128)}, f32[2,64,2,512]{3,2,1,0:T(2,128)}) fusion(f32[3,64,32,512]{3,2,1,0:T(8,128)} %pot.1), kind=kLoop, calls=%fused_computation.8 | loop fusion | bytes 2097152 | tf_op jit(solution)/shard_map/slice | solution.py:444
  18.6 28.5 %shard_map.60 = (f32[2,2,32,512]{3,2,1,0:T(8,128)}, f32[2,2,32,512]{3,2,1,0:T(8,128)}, f32[2,64,2,512]{3,2,1,0:T(2,128)}, f32[2,64,2,512]{3,2,1,0:T(2,128)}) custom-call(f32[2,2,32,512]{3,2,1,0:T(8,128)} %get-tuple-element.78.zup, f32[2,2,32,512]{3,2,1,0:T(8,128)} %get-tuple-element.77.zdown, f32[2,64,2,512]{3,2,1,0:T(2,128)} %get-tuple-element.76.xup, ...), custom_call_target="tpu_custom_call" | custom-call | tf_op jit(solution)/shard_map/pallas_call | solution.py:433
  47.1 25.7 %shard_map.61 = (f32[64,32,512]{2,1,0:T(8,128)}, f32[64,32,512]{2,1,0:T(8,128)}, f32[64,32,512]{2,1,0:T(8,128)}, f32[32,512]{1,0:T(8,128)S(1)}, f32[32,512]{1,0:T(8,128)}, /*index=5*/f32[32,512]{1,0:T(8,128)}) custom-call(f32[64]{0:T(128)} %multiply_cosine_fusion.1.zcos, f32[3,64,32,512]{3,2,1,0:T(8,128)} %pot.1, f32[2,2,32,512]{3,2,1,0:T(8,128)} %get-tuple-element.60.zlow, ...), custom_call_target="tpu_custom_call" | custom-call | tf_op jit(solution)/shard_map/pallas_call | solution.py:456
  72.9 0.0 copy-start
  72.9 61.0 %shard_map.62 = (f32[2,22,32,512]{3,2,1,0:T(8,128)S(1)}, f32[32,512]{1,0:T(8,128)S(1)}, f32[8,128]{1,0:T(8,128)}) custom-call(f32[64,32,512]{2,1,0:T(8,128)} %get-tuple-element.64.q_ref, f32[64,32,512]{2,1,0:T(8,128)} %get-tuple-element.65.u_ref, f32[64,32,512]{2,1,0:T(8,128)} %get-tuple-element.66.sum_ref, f32[32,512]{1,0:T(8,128)S(1)} %get-tuple-element.67.total_ref, ...), custom_call_target="tpu_custom_call" | custom-call | tf_op jit(solution)/shard_map/pallas_call | solution.py:471
  133.9 1.3 reduce_max.9
  135.9 0.0 copy-done
  135.9 9.9 %conditional.1 = (f32[16,2,32,512]{3,2,1,0:T(8,128)}) conditional(s32[]{:T(128)} %convert_element_type.32, (s32[]{:T(128)}, f32[32,512]{1,0:T(8,128)S(1)}, f32[64]{0:T(128)S(1)}, f32[64]{0:T(128)S(1)}, f32[64,32,512]{2,1,0:T(8,128)}, /*index=5*/f32[64,32,512]{2,1,0:T(8,128)}, f32[64,32,512]{2,1,0:T(8,128)}) %tuple.14, (s32[]{:T(128)}, ...), branch_computations={%region_1.4_spmd, %region_4.5_spmd} | conditional | flops 114692 | bytes 32112700 | solution.py:543
  135.9 0.6 dynamic_slice.6.index
  136.5 0.6 dynamic_slice.7.lam
  137.1 0.7 dynamic_slice.8.weight
  137.7 8.0 %branch_1_fun.1 = f32[16,2,32,512]{3,2,1,0:T(8,128)} custom-call(s32[16]{0:T(128)} %dynamic_slice.6.index, f32[16]{0:T(128)} %dynamic_slice.7.lam, f32[16]{0:T(128)} %dynamic_slice.8.weight, f32[1408]{0:T(1024)} %constant.45.clone.1.table, f32[2,22,32,512]{3,2,1,0:T(8,128)S(1)} %get-tuple-element.43.moments, f32[32,512]{1,0:T(8,128)S(1)} %get-tuple-element.44.depth_ref), custom_call_target="tpu_custom_call" | custom-call | tf_op jit(solution)/shard_map/cond/branch_1_fun/pallas_call | solution.py:511
  145.7 0.6 copy.11
Async XLA Ops:
  72.9 63.0 %copy-start = (s32[64]{0:T(128)S(1)}, s32[64]{0:T(128)}, u32[]{:S(2)}) copy-start(s32[64]{0:T(128)} %param.7) | copy-start | bytes 772

commit v3 on v2

--- a/solution.py
+++ b/solution.py
@@ -189,8 +189,8 @@
 
 def moment_kernel(
     middle, q_ref, u_ref, sum_ref, total_ref, high_ref, low_ref,
-    out, depth_out, far_out,
-    others, start_ref, own, near, part, across, far, far_depth, far_mid, far_tile,
+    out, depth_out, far_out, start_ref,
+    others, own, near, part, across, far, far_depth, far_mid, far_tile,
     carry_send, carry_recv, far_send, far_recv, tile_send, tile_recv,
     near_send, near_recv, cross_send, cross_recv, back_send, back_recv,
 ):
@@ -351,11 +351,11 @@
             for item in tiles_far:
                 item.start()
 
-        pl.when(jnp.logical_and(g >= 1, g <= chunks))(lambda: sum_chip(g - 1))
-        pl.when(g >= 2)(lambda: sum_all(g - 2))
+        pl.when(g < chunks)(lambda: sum_chip(g))
+        pl.when(g >= 1)(lambda: sum_all(g - 1))
         return carry
 
-    lax.fori_loop(0, chunks + 2, lap, 0)
+    lax.fori_loop(0, chunks + 1, lap, 0)
     reach = far_mid[...]
     for k, item in enumerate(tiles_far):
         item.wait()
@@ -367,13 +367,14 @@
 
 def channel_kernel(index, lam, weight, table, moments, depth_ref, out):
     rows, _, strip, width = out.shape
+    first_row = lax.axis_index("depth") * rows
 
     def band(step, carry):
         place = pl.ds(pl.multiple_of(step * 8, 8), 8)
         half = 0.5 * depth_ref[place]
 
         def one(row, carry):
-            base = index[row] * TERMS
+            base = index[first_row + row] * TERMS
             real_part = table[base] * moments[0, 0, place]
             imag_part = table[base] * moments[1, 0, place]
             for j in range(1, TERMS):
@@ -386,9 +387,9 @@
                 else:
                     real_part = real_part - second
                     imag_part = imag_part + first
-            cosine, sine = turn_of_phase(2.0 * lam[row] * half)
-            out[row, 0, place] = (real_part * cosine - imag_part * sine) * weight[row]
-            out[row, 1, place] = (real_part * sine + imag_part * cosine) * weight[row]
+            cosine, sine = turn_of_phase(2.0 * lam[first_row + row] * half)
+            out[row, 0, place] = (real_part * cosine - imag_part * sine) * weight[first_row + row]
+            out[row, 1, place] = (real_part * sine + imag_part * cosine) * weight[first_row + row]
             return carry
 
         return lax.fori_loop(0, rows, one, carry)
@@ -468,18 +469,18 @@
     small = (8, 128)
     dma = pltpu.SemaphoreType.DMA
     pair = [dma((depth_count - 1,))] * 4 + [dma((tile_count - 1,))] * 2
-    moments, faraday_depth, farthest = pl.pallas_call(
+    moments, faraday_depth, farthest, start = pl.pallas_call(
         functools.partial(moment_kernel, float(middle)),
         out_shape=(
             jax.ShapeDtypeStruct((2, TERMS, strip, width), jnp.float32),
             flat,
             jax.ShapeDtypeStruct(small, jnp.float32),
+            flat,
         ),
         in_specs=[vmem] * 6,
-        out_specs=(vmem,) * 3,
+        out_specs=(vmem,) * 4,
         scratch_shapes=[
             pltpu.VMEM((depth_count - 1, strip, width), jnp.float32),
-            pltpu.VMEM((strip, width), jnp.float32),
             pltpu.VMEM((chunks, 2) + half, jnp.float32),
             pltpu.VMEM((chunks,) + half, jnp.float32),
             pltpu.VMEM((chunks,) + half, jnp.float32),
@@ -504,9 +505,6 @@
     weight = 1.0 / (freq * jnp.sqrt(jnp.float32(slab * depth_count)))
     rows = NCH // depth_count
 
-    def own(values):
-        return lax.dynamic_slice_in_dim(values, depth_place * rows, rows)
-
     def by_series(_):
         return pl.pallas_call(
             channel_kernel,
@@ -515,18 +513,16 @@
             out_specs=vmem,
             compiler_params=params,
         )(
-            own(channel_index),
-            own(lam2),
-            own(weight),
+            channel_index,
+            lam2,
+            weight,
             jnp.asarray(table.reshape(-1)),
             moments,
             faraday_depth,
         )
 
     def by_sum(_):
-        totals = lax.all_gather(own_total, "depth")
-        before = (jnp.arange(depth_count) < depth_place)[:, None, None]
-        nearer = jnp.sum(jnp.where(before, totals, 0.0), axis=0)
+        nearer = start + 0.5 * faraday_depth
         whole = pl.BlockSpec((slab, strip, width), lambda c: (0, 0, 0))
         sums = pl.pallas_call(
             direct_kernel,
@@ -538,7 +534,8 @@
             out_specs=pl.BlockSpec((1, 2, strip, width), lambda c: (c, 0, 0, 0)),
             compiler_params=params,
         )(lam2, weight, stokes_q, stokes_u, slab_sums, nearer)
-        return lax.psum_scatter(sums, "depth", scatter_dimension=0, tiled=True)
+        sums = sums.reshape(depth_count, rows, 2, strip, width)
+        return jnp.sum(lax.all_to_all(sums, "depth", 0, 0), axis=0)
 
     pol_spectra = lax.cond(farthest <= REACH, by_series, by_sum, 0)
     return (pol_spectra, faraday_depth)

time: 153 us -> 135 us (0.88)
  between operations: 14.7 us -> 1.32 us
  Pallas kernels: 123 us -> 120 us
  local copies, waits for them, and re-layouts: 9.39 us -> 7.56 us
    pallas_call x1, Pallas kernels: 61 us -> 57.9 us  [body(): pl.pallas_call(functools.partial(moment_kernel, float(middle)), out_shape...]
    dynamic_slice x3 -> x0, local copies, waits for them, and re-layouts: 1.83 us -> none  [own(): return lax.dynamic_slice_in_dim(values, depth_place * rows, rows)]
where the time goes in v3:
time: 135 us
  Pallas kernels  120 us (89%)
  local copies, waits for them, and re-layouts  7.56 us (6%)
  other arithmetic  5.78 us (4%)
    pallas_call x1, Pallas kernels, body(): pl.pallas_call(functools.partial(moment_kernel, float(middle)), out_shape...  57.9 us
    pallas_call x1, Pallas kernels, body(): pl.pallas_call(halo_kernel, out_shape=tuple((jax.ShapeDtypeStruct(shape,...  28.5 us
    pallas_call x1, Pallas kernels, body(): pl.pallas_call(field_kernel, out_shape=(plane, plane, plane, flat, flat,...  25.7 us
    pallas_call x1, Pallas kernels, by_series(): pl.pallas_call(channel_kernel, out_shape=jax.ShapeDtypeStruct((rows, 2, s...  7.93 us
    slice x1, local copies, waits for them, and re-layouts, body(): potential[1:3, :, :2]  3.72 us

profile of v3, /device:TPU:0, one launch (start us, length us, event | category | flops | bytes accessed | tf_op | source)
XLA Modules:
  0.0 134.8 jit_solution(2052038609119616259)
XLA Ops:
  0.6 0.7 multiply_divide_fusion
  1.3 1.4 %fusion.2 = (s32[1]{0:T(128)}, s32[1]{0:T(128)}, s32[1]{0:T(128)}) fusion(s32[3]{0:T(128)} %param.8), kind=kLoop, calls=%fused_computation.9 | loop fusion | bytes 24 | tf_op jit(solution)/shard_map/slice | solution.py:451
  2.7 1.3 multiply_cosine_fusion.1.zcos
  3.9 1.3 multiply_sine_fusion.ysin
  5.2 1.2 multiply_cosine_fusion.xcos
  6.5 1.9 %fusion.1 = (f32[2,2,32,512]{3,2,1,0:T(8,128)}, f32[2,2,32,512]{3,2,1,0:T(8,128)}) fusion(f32[3,64,32,512]{3,2,1,0:T(8,128)} %pot.1), kind=kLoop, calls=%fused_computation.8 | loop fusion | bytes 1048576 | tf_op jit(solution)/shard_map/slice | solution.py:443
  8.3 3.7 %fusion = (f32[2,64,2,512]{3,2,1,0:T(2,128)}, f32[2,64,2,512]{3,2,1,0:T(2,128)}) fusion(f32[3,64,32,512]{3,2,1,0:T(8,128)} %pot.1), kind=kLoop, calls=%fused_computation.7 | loop fusion | bytes 2097152 | tf_op jit(solution)/shard_map/slice | solution.py:445
  12.1 28.5 %shard_map.60 = (f32[2,2,32,512]{3,2,1,0:T(8,128)}, f32[2,2,32,512]{3,2,1,0:T(8,128)}, f32[2,64,2,512]{3,2,1,0:T(2,128)}, f32[2,64,2,512]{3,2,1,0:T(2,128)}) custom-call(f32[2,2,32,512]{3,2,1,0:T(8,128)} %get-tuple-element.77.zup, f32[2,2,32,512]{3,2,1,0:T(8,128)} %get-tuple-element.76.zdown, f32[2,64,2,512]{3,2,1,0:T(2,128)} %get-tuple-element.75.xup, ...), custom_call_target="tpu_custom_call" | custom-call | tf_op jit(solution)/shard_map/pallas_call | solution.py:434
  40.6 25.7 %shard_map.61 = (f32[64,32,512]{2,1,0:T(8,128)}, f32[64,32,512]{2,1,0:T(8,128)}, f32[64,32,512]{2,1,0:T(8,128)}, f32[32,512]{1,0:T(8,128)}, f32[32,512]{1,0:T(8,128)}, /*index=5*/f32[32,512]{1,0:T(8,128)}) custom-call(f32[64]{0:T(128)} %multiply_cosine_fusion.1.zcos, f32[3,64,32,512]{3,2,1,0:T(8,128)} %pot.1, f32[2,2,32,512]{3,2,1,0:T(8,128)} %get-tuple-element.58.zlow, ...), custom_call_target="tpu_custom_call" | custom-call | tf_op jit(solution)/shard_map/pallas_call | solution.py:457
  66.3 0.0 copy-start
  66.3 57.9 %shard_map.62 = (f32[2,22,32,512]{3,2,1,0:T(8,128)S(1)}, f32[32,512]{1,0:T(8,128)S(1)}, f32[8,128]{1,0:T(8,128)}, f32[32,512]{1,0:T(8,128)S(1)}) custom-call(f32[64,32,512]{2,1,0:T(8,128)} %get-tuple-element.62.q_ref, f32[64,32,512]{2,1,0:T(8,128)} %get-tuple-element.63.u_ref, f32[64,32,512]{2,1,0:T(8,128)} %get-tuple-element.64.sum_ref, ...), custom_call_target="tpu_custom_call" | custom-call | tf_op jit(solution)/shard_map/pallas_call | solution.py:472
  124.2 1.3 reduce_max.9
  126.2 0.0 copy-done
  126.2 7.9 %conditional.1 = (f32[16,2,32,512]{3,2,1,0:T(8,128)}) conditional(s32[]{:T(128)} %convert_element_type.32, (f32[32,512]{1,0:T(8,128)S(1)}, f32[32,512]{1,0:T(8,128)S(1)}, f32[64]{0:T(128)S(1)}, f32[64]{0:T(128)S(1)}, f32[64,32,512]{2,1,0:T(8,128)}, /*index=5*/f32[64,32,512]{2,1,0:T(8,128)}, f32[64,32,512]{2,1,0:T(8,128)}) %tuple.14, ...), branch_computations={%region_1.0_spmd, %region_3.0_spmd} | conditional | flops 1605632 | bytes 27459596 | solution.py:540
  126.2 7.9 %branch_1_fun.1 = f32[16,2,32,512]{3,2,1,0:T(8,128)} custom-call(s32[64]{0:T(128)S(1)} %get-tuple-element.36.index, f32[64]{0:T(128)S(1)} %get-tuple-element.37.lam, f32[64]{0:T(128)S(1)} %get-tuple-element.38.weight, f32[1408]{0:T(1024)} %constant.41.clone.1.table, f32[2,22,32,512]{3,2,1,0:T(8,128)S(1)} %get-tuple-element.40.moments, ...), custom_call_target="tpu_custom_call" | custom-call | tf_op jit(solution)/shard_map/cond/branch_1_fun/pallas_call | solution.py:509
  134.2 0.6 copy.11
Async XLA Ops:
  66.3 59.9 %copy-start = (s32[64]{0:T(128)S(1)}, s32[64]{0:T(128)}, u32[]{:S(2)}) copy-start(s32[64]{0:T(128)} %param.7) | copy-start | bytes 772

commit v4 on v3

--- a/solution.py
+++ b/solution.py
@@ -72,65 +72,13 @@
     return turn(rest * (1.0 / two_pi))
 
 
-def field_kernel(zcos, pot, zlow, zhigh, xlow, xhigh, xcos, ysin, q_out, u_out, sum_out, total_out, high_out, low_out):
+def field_kernel(
+    zcos, pot, zup, zdown, xup, xdown, xcos, ysin,
+    q_out, u_out, sum_out, total_out, high_out, low_out,
+    zlow, zhigh, xlow, xhigh, send, recv,
+):
     slab, strip, width = sum_out.shape
-    column = lax.broadcasted_iota(jnp.int32, (strip, width), 1)
-    ybase = jnp.broadcast_to(1.0 + 0.3 * ysin[...], (strip, width))
-    xhalf = jnp.broadcast_to(0.5 * xcos[...], (strip, width))
-
-    def along_last(v):
-        up1 = jnp.where(column < width - 1, pltpu.roll(v, width - 1, 1), 0.0)
-        up2 = jnp.where(column < width - 2, pltpu.roll(v, width - 2, 1), 0.0)
-        down1 = jnp.where(column >= 1, pltpu.roll(v, 1, 1), 0.0)
-        down2 = jnp.where(column >= 2, pltpu.roll(v, 2, 1), 0.0)
-        return (8.0 * (up1 - down1) - (up2 - down2)) * (1.0 / 12.0)
-
-    def along_mid(component, z):
-        low = xlow[component - 1, z]
-        high = xhigh[component - 1, z]
-        v = jnp.concatenate([low, pot[component, z], high], axis=0)
-        return (8.0 * (v[3 : strip + 3] - v[1 : strip + 1]) - (v[4 : strip + 4] - v[0:strip])) * (
-            1.0 / 12.0
-        )
-
-    def along_lead(component, z, edge):
-        def plane(step):
-            if edge is None:
-                return pot[component, z + step]
-            place = edge + step
-            if place < 0:
-                return zlow[component, place + 2]
-            if place >= slab:
-                return zhigh[component, place - slab]
-            return pot[component, place]
-
-        return (8.0 * (plane(1) - plane(-1)) - (plane(2) - plane(-2))) * (1.0 / 12.0)
-
-    def one(z, state, edge=None):
-        before, high, low = state
-        field_x = along_last(pot[2, z]) - along_lead(1, z, edge)
-        field_y = along_lead(0, z, edge) - along_mid(2, z)
-        field_z = along_mid(1, z) - along_last(pot[0, z])
-        density = ybase + zcos[z] * xhalf
-        q_out[z] = density * (field_y * field_y - field_x * field_x)
-        u_out[z] = -2.0 * density * field_x * field_y
-        now = before + density * field_z
-        sum_out[z] = now
-        return now, jnp.maximum(high, now), jnp.minimum(low, now)
-
-    zero = jnp.zeros((strip, width), jnp.float32)
-    state = (zero, zero, zero)
-    for z in (0, 1):
-        state = one(z, state, z)
-    state = lax.fori_loop(2, slab - 2, one, state)
-    for z in (slab - 2, slab - 1):
-        state = one(z, state, z)
-    total_out[...] = faraday_coef * state[0]
-    high_out[...] = faraday_coef * state[1]
-    low_out[...] = faraday_coef * state[2]
-
-
-def halo_kernel(zup, zdown, xup, xdown, zlow, zhigh, xlow, xhigh, send, recv):
+    bands = strip // 8
     barrier = pltpu.get_barrier_semaphore()
     plan = []
     for order, (axis, up, down, low, high) in enumerate(
@@ -154,14 +102,13 @@
             barrier, inc=1, device_id={axis: index}, device_id_type=pl.DeviceIdType.MESH
         )
 
+    count = 0
     for axis, place, last, above, below, low, high in plan:
         pl.when(place > 0)(functools.partial(signal, axis, place - 1))
         pl.when(place < last)(functools.partial(signal, axis, place + 1))
-    count = 0
-    for axis, place, last, above, below, low, high in plan:
         count = count + (place + last - 1) // last + (2 * last - place - 1) // last
     pl.semaphore_wait(barrier, count)
-    for axis, place, last, above, below, low, high in reversed(plan):
+    for axis, place, last, above, below, low, high in plan:
         pl.when(place < last)(above.start)
         pl.when(place > 0)(below.start)
     for axis, place, last, above, below, low, high in plan:
@@ -174,8 +121,7 @@
         def _():
             high[...] = jnp.zeros_like(high)
 
-    for axis, place, last, above, below, low, high in plan:
-
+    def arrive(axis, place, last, above, below, low, high):
         @pl.when(place < last)
         def _():
             above.wait_send()
@@ -185,6 +131,80 @@
         def _():
             below.wait_send()
             above.wait_recv()
+
+    column = lax.broadcasted_iota(jnp.int32, (8, width), 1)
+
+    def along_last(v):
+        up1 = jnp.where(column < width - 1, pltpu.roll(v, width - 1, 1), 0.0)
+        up2 = jnp.where(column < width - 2, pltpu.roll(v, width - 2, 1), 0.0)
+        down1 = jnp.where(column >= 1, pltpu.roll(v, 1, 1), 0.0)
+        down2 = jnp.where(column >= 2, pltpu.roll(v, 2, 1), 0.0)
+        return (8.0 * (up1 - down1) - (up2 - down2)) * (1.0 / 12.0)
+
+    def one_band(band):
+        rows = slice(8 * band, 8 * band + 8)
+        ybase = jnp.broadcast_to(1.0 + 0.3 * ysin[...], (8, width))
+        xhalf = jnp.broadcast_to(0.5 * xcos[rows], (8, width))
+
+        def along_mid(component, z):
+            if band == 0:
+                v = jnp.concatenate([xlow[component - 1, z], pot[component, z, 0:16]], axis=0)
+                at = 0
+            elif band == bands - 1:
+                v = jnp.concatenate(
+                    [pot[component, z, strip - 16 : strip], xhigh[component - 1, z]], axis=0
+                )
+                at = 6
+            else:
+                v = pot[component, z, 8 * band - 8 : 8 * band + 16]
+                at = 6
+            return (
+                8.0 * (v[at + 3 : at + 11] - v[at + 1 : at + 9])
+                - (v[at + 4 : at + 12] - v[at : at + 8])
+            ) * (1.0 / 12.0)
+
+        def along_lead(component, z, edge):
+            def plane(step):
+                if edge is None:
+                    return pot[component, z + step, rows]
+                place = edge + step
+                if place < 0:
+                    return zlow[component, place + 2, rows]
+                if place >= slab:
+                    return zhigh[component, place - slab, rows]
+                return pot[component, place, rows]
+
+            return (8.0 * (plane(1) - plane(-1)) - (plane(2) - plane(-2))) * (1.0 / 12.0)
+
+        def one(z, state, edge=None):
+            before, high, low = state
+            field_x = along_last(pot[2, z, rows]) - along_lead(1, z, edge)
+            field_y = along_lead(0, z, edge) - along_mid(2, z)
+            field_z = along_mid(1, z) - along_last(pot[0, z, rows])
+            density = ybase + zcos[z] * xhalf
+            q_out[z, rows] = density * (field_y * field_y - field_x * field_x)
+            u_out[z, rows] = -2.0 * density * field_x * field_y
+            now = before + density * field_z
+            sum_out[z, rows] = now
+            return now, jnp.maximum(high, now), jnp.minimum(low, now)
+
+        zero = jnp.zeros((8, width), jnp.float32)
+        state = (zero, zero, zero)
+        for z in (0, 1):
+            state = one(z, state, z)
+        state = lax.fori_loop(2, slab - 2, one, state)
+        for z in (slab - 2, slab - 1):
+            state = one(z, state, z)
+        total_out[rows] = faraday_coef * state[0]
+        high_out[rows] = faraday_coef * state[1]
+        low_out[rows] = faraday_coef * state[2]
+
+    arrive(*plan[0])
+    for band in range(1, bands - 1):
+        one_band(band)
+    arrive(*plan[1])
+    for band in (0, bands - 1):
+        one_band(band)
 
 
 def moment_kernel(
@@ -431,19 +451,6 @@
     depth_place = lax.axis_index("depth")
     slab, strip, width = (potential.shape[1], potential.shape[2], potential.shape[3])
     shapes = [(2, 2, strip, width)] * 2 + [(2, slab, 2, width)] * 2
-    zlow, zhigh, xlow, xhigh = pl.pallas_call(
-        halo_kernel,
-        out_shape=tuple(jax.ShapeDtypeStruct(shape, jnp.float32) for shape in shapes),
-        in_specs=[vmem] * 4,
-        out_specs=(vmem,) * 4,
-        scratch_shapes=[pltpu.SemaphoreType.DMA((4,)), pltpu.SemaphoreType.DMA((4,))],
-        compiler_params=pltpu.CompilerParams(collective_id=0, has_side_effects=True),
-    )(
-        potential[0:2, slab - 2 :],
-        potential[0:2, :2],
-        potential[1:3, :, strip - 2 :],
-        potential[1:3, :, :2],
-    )
     zstart = depth_place * slab
     xstart = lax.axis_index("tile") * strip
     zpos = (zstart + jnp.arange(slab, dtype=jnp.int32) + patch_offsets[0]).astype(jnp.float32)
@@ -459,8 +466,21 @@
         out_shape=(plane, plane, plane, flat, flat, flat),
         in_specs=[smem] + [vmem] * 7,
         out_specs=(vmem,) * 6,
-        compiler_params=params,
-    )(zcos, potential, zlow, zhigh, xlow, xhigh, xcos, ysin)
+        scratch_shapes=[pltpu.VMEM(shape, jnp.float32) for shape in shapes]
+        + [pltpu.SemaphoreType.DMA((4,))] * 2,
+        compiler_params=pltpu.CompilerParams(
+            collective_id=0, has_side_effects=True, vmem_limit_bytes=60 * 1024 * 1024
+        ),
+    )(
+        zcos,
+        potential,
+        potential[0:2, slab - 2 :],
+        potential[0:2, :2],
+        potential[1:3, :, strip - 2 :],
+        potential[1:3, :, :2],
+        xcos,
+        ysin,
+    )
 
     middle, table = series_table()
     tile_count = lax.axis_size("tile")

time: 135 us -> 130 us (0.963)
  Pallas kernels: 120 us -> 115 us
    pallas_call x1 -> x0, Pallas kernels: 28.5 us -> none  [body(): pl.pallas_call(halo_kernel, out_shape=tuple((jax.ShapeDtypeStruct(shape,...]
    pallas_call x1, Pallas kernels: 25.7 us -> 49.4 us  [body(): pl.pallas_call(field_kernel, out_shape=(plane, plane, plane, flat, flat,...]
where the time goes in v4:
time: 130 us
  Pallas kernels  115 us (88%)
  local copies, waits for them, and re-layouts  7.57 us (6%)
  other arithmetic  5.82 us (4%)
  between operations  1.32 us (1%)
    pallas_call x1, Pallas kernels, body(): pl.pallas_call(functools.partial(moment_kernel, float(middle)), out_shape...  57.9 us
    pallas_call x1, Pallas kernels, body(): pl.pallas_call(field_kernel, out_shape=(plane, plane, plane, flat, flat,...  49.4 us
    pallas_call x1, Pallas kernels, by_series(): pl.pallas_call(channel_kernel, out_shape=jax.ShapeDtypeStruct((rows, 2, s...  7.93 us
    slice x1, local copies, waits for them, and re-layouts, body(): potential[1:3, :, :2]  3.71 us

profile of v4, /device:TPU:0, one launch (start us, length us, event | category | flops | bytes accessed | tf_op | source)
XLA Modules:
  0.0 130.0 jit_solution(8949946013693269913)
XLA Ops:
  0.6 0.7 multiply_divide_fusion
  1.3 1.4 %fusion.2 = (s32[1]{0:T(128)}, s32[1]{0:T(128)}, s32[1]{0:T(128)}) fusion(s32[3]{0:T(128)} %param.8), kind=kLoop, calls=%fused_computation.9 | loop fusion | bytes 24 | tf_op jit(solution)/shard_map/slice | solution.py:458
  2.7 1.3 multiply_cosine_fusion.1.zcos
  3.9 1.3 %multiply_sine_fusion.ysin = f32[1,512]{1,0:T(1,128)} fusion(s32[]{:T(128)} %bitcast.3), kind=kLoop, calls=%fused_computation.2 | loop fusion | flops 1536 | bytes 2052 | tf_op jit(solution)/shard_map/sin | solution.py:461
  5.2 1.3 %multiply_cosine_fusion.xcos = f32[32,1]{1,0:T(8,128)} fusion(s32[]{:T(128)S(6)} %mul.52, s32[]{:T(128)} %bitcast.2), kind=kLoop, calls=%fused_computation.1 | loop fusion | flops 128 | bytes 136 | tf_op jit(solution)/shard_map/cos | solution.py:460
  6.5 1.9 %fusion.1 = (f32[2,2,32,512]{3,2,1,0:T(8,128)}, f32[2,2,32,512]{3,2,1,0:T(8,128)}) fusion(f32[3,64,32,512]{3,2,1,0:T(8,128)} %pot.1), kind=kLoop, calls=%fused_computation.8 | loop fusion | bytes 1048576 | tf_op jit(solution)/shard_map/slice | solution.py:478
  8.4 3.7 %fusion = (f32[2,64,2,512]{3,2,1,0:T(2,128)}, f32[2,64,2,512]{3,2,1,0:T(2,128)}) fusion(f32[3,64,32,512]{3,2,1,0:T(8,128)} %pot.1), kind=kLoop, calls=%fused_computation.7 | loop fusion | bytes 2097152 | tf_op jit(solution)/shard_map/slice | solution.py:480
  12.1 49.4 %shard_map.60 = (f32[64,32,512]{2,1,0:T(8,128)}, f32[64,32,512]{2,1,0:T(8,128)}, f32[64,32,512]{2,1,0:T(8,128)}, f32[32,512]{1,0:T(8,128)}, f32[32,512]{1,0:T(8,128)}, /*index=5*/f32[32,512]{1,0:T(8,128)}) custom-call(f32[64]{0:T(128)} %multiply_cosine_fusion.1.zcos, f32[3,64,32,512]{3,2,1,0:T(8,128)} %pot.1, f32[2,2,32,512]{3,2,1,0:T(8,128)} %get-tuple-element.69.zup, ...), custom_call_target="tpu_custom_call" | custom-call | tf_op jit(solution)/shard_map/pallas_call | solution.py:464
  61.5 0.0 copy-start
  61.5 57.9 %shard_map.61 = (f32[2,22,32,512]{3,2,1,0:T(8,128)S(1)}, f32[32,512]{1,0:T(8,128)S(1)}, f32[8,128]{1,0:T(8,128)}, f32[32,512]{1,0:T(8,128)S(1)}) custom-call(f32[64,32,512]{2,1,0:T(8,128)} %get-tuple-element.54.q_ref, f32[64,32,512]{2,1,0:T(8,128)} %get-tuple-element.55.u_ref, f32[64,32,512]{2,1,0:T(8,128)} %get-tuple-element.56.sum_ref, ...), custom_call_target="tpu_custom_call" | custom-call | tf_op jit(solution)/shard_map/pallas_call | solution.py:492
  119.5 1.3 reduce_max.9
  121.4 0.0 copy-done
  121.4 7.9 %conditional.1 = (f32[16,2,32,512]{3,2,1,0:T(8,128)}) conditional(s32[]{:T(128)} %convert_element_type.32, (f32[32,512]{1,0:T(8,128)S(1)}, f32[32,512]{1,0:T(8,128)S(1)}, f32[64]{0:T(128)S(1)}, f32[64]{0:T(128)S(1)}, f32[64,32,512]{2,1,0:T(8,128)}, /*index=5*/f32[64,32,512]{2,1,0:T(8,128)}, f32[64,32,512]{2,1,0:T(8,128)}) %tuple.14, ...), branch_computations={%region_1.0_spmd, %region_3.0_spmd} | conditional | flops 1605632 | bytes 27459596 | solution.py:560
  121.4 7.9 %branch_1_fun.1 = f32[16,2,32,512]{3,2,1,0:T(8,128)} custom-call(s32[64]{0:T(128)S(1)} %get-tuple-element.36.index, f32[64]{0:T(128)S(1)} %get-tuple-element.37.lam, f32[64]{0:T(128)S(1)} %get-tuple-element.38.weight, f32[1408]{0:T(1024)} %constant.41.clone.1.table, f32[2,22,32,512]{3,2,1,0:T(8,128)S(1)} %get-tuple-element.40.moments, ...), custom_call_target="tpu_custom_call" | custom-call | tf_op jit(solution)/shard_map/cond/branch_1_fun/pallas_call | solution.py:529
  129.4 0.6 copy.11
Async XLA Ops:
  61.5 59.9 %copy-start = (s32[64]{0:T(128)S(1)}, s32[64]{0:T(128)}, u32[]{:S(2)}) copy-start(s32[64]{0:T(128)} %param.7) | copy-start | bytes 772

commit v5 on v4

--- a/solution.py
+++ b/solution.py
@@ -146,13 +146,18 @@
         ybase = jnp.broadcast_to(1.0 + 0.3 * ysin[...], (8, width))
         xhalf = jnp.broadcast_to(0.5 * xcos[rows], (8, width))
 
+        def pair_of(ref, component, z):
+            return jnp.concatenate([ref[component, k, pl.ds(z, 1)] for k in range(2)], axis=0)
+
         def along_mid(component, z):
             if band == 0:
-                v = jnp.concatenate([xlow[component - 1, z], pot[component, z, 0:16]], axis=0)
+                v = jnp.concatenate(
+                    [pair_of(xlow, component - 1, z), pot[component, z, 0:16]], axis=0
+                )
                 at = 0
             elif band == bands - 1:
                 v = jnp.concatenate(
-                    [pot[component, z, strip - 16 : strip], xhigh[component - 1, z]], axis=0
+                    [pot[component, z, strip - 16 : strip], pair_of(xhigh, component - 1, z)], axis=0
                 )
                 at = 6
             else:
@@ -450,7 +455,7 @@
     depth_count = lax.axis_size("depth")
     depth_place = lax.axis_index("depth")
     slab, strip, width = (potential.shape[1], potential.shape[2], potential.shape[3])
-    shapes = [(2, 2, strip, width)] * 2 + [(2, slab, 2, width)] * 2
+    shapes = [(2, 2, strip, width)] * 2 + [(2, 2, slab, width)] * 2
     zstart = depth_place * slab
     xstart = lax.axis_index("tile") * strip
     zpos = (zstart + jnp.arange(slab, dtype=jnp.int32) + patch_offsets[0]).astype(jnp.float32)
@@ -476,8 +481,8 @@
         potential,
         potential[0:2, slab - 2 :],
         potential[0:2, :2],
-        potential[1:3, :, strip - 2 :],
-        potential[1:3, :, :2],
+        potential[1:3, :, strip - 2 :].transpose(0, 2, 1, 3),
+        potential[1:3, :, :2].transpose(0, 2, 1, 3),
         xcos,
         ysin,
     )

time: 130 us -> 130 us (level)
  no operation moved by 1% of the time
where the time goes in v5:
time: 130 us
  Pallas kernels  115 us (88%)
  local copies, waits for them, and re-layouts  7.74 us (6%)
  other arithmetic  5.71 us (4%)
  between operations  1.33 us (1%)
    pallas_call x1, Pallas kernels, body(): pl.pallas_call(functools.partial(moment_kernel, float(middle)), out_shape...  57.9 us
    pallas_call x1, Pallas kernels, body(): pl.pallas_call(field_kernel, out_shape=(plane, plane, plane, flat, flat,...  49.4 us
    pallas_call x1, Pallas kernels, by_series(): pl.pallas_call(channel_kernel, out_shape=jax.ShapeDtypeStruct((rows, 2, s...  7.93 us
    slice x1, local copies, waits for them, and re-layouts, body(): potential[1:3, :, :2].transpose(0, 2, 1, 3)  2.75 us

profile of v5, /device:TPU:0, one launch (start us, length us, event | category | flops | bytes accessed | tf_op | source)
XLA Modules:
  0.0 130.0 jit_solution(6757942167274795483)
XLA Ops:
  0.6 0.7 multiply_divide_fusion
  1.3 1.4 %fusion.2 = (s32[1]{0:T(128)}, s32[1]{0:T(128)}, s32[1]{0:T(128)}) fusion(s32[3]{0:T(128)} %param.8), kind=kLoop, calls=%fused_computation.11 | loop fusion | bytes 24 | tf_op jit(solution)/shard_map/slice | solution.py:463
  2.7 1.2 multiply_cosine_fusion.1.zcos
  3.9 1.3 %multiply_sine_fusion.ysin = f32[1,512]{1,0:T(1,128)} fusion(s32[]{:T(128)} %bitcast.5), kind=kLoop, calls=%fused_computation.4 | loop fusion | flops 1536 | bytes 2052 | tf_op jit(solution)/shard_map/sin | solution.py:466
  5.2 1.2 multiply_cosine_fusion.xcos
  6.4 1.9 %fusion.1 = (f32[2,2,32,512]{3,2,1,0:T(8,128)}, f32[2,2,32,512]{3,2,1,0:T(8,128)}) fusion(f32[3,64,32,512]{3,2,1,0:T(8,128)} %pot.1), kind=kLoop, calls=%fused_computation.10 | loop fusion | bytes 1048576 | tf_op jit(solution)/shard_map/slice | solution.py:483
  8.3 2.7 %fusion = (f32[2,64,2,512]{3,2,1,0:T(2,128)S(1)}, f32[2,64,2,512]{3,2,1,0:T(2,128)S(1)}) fusion(f32[3,64,32,512]{3,2,1,0:T(8,128)} %pot.1), kind=kLoop, calls=%fused_computation.9 | loop fusion | bytes 2097152 | tf_op jit(solution)/shard_map/slice | solution.py:485
  11.0 1.1 copy_bitcast_fusion
  12.2 49.4 %shard_map.60 = (f32[64,32,512]{2,1,0:T(8,128)}, f32[64,32,512]{2,1,0:T(8,128)}, f32[64,32,512]{2,1,0:T(8,128)}, f32[32,512]{1,0:T(8,128)}, f32[32,512]{1,0:T(8,128)}, /*index=5*/f32[32,512]{1,0:T(8,128)}) custom-call(f32[64]{0:T(128)} %multiply_cosine_fusion.1.zcos, f32[3,64,32,512]{3,2,1,0:T(8,128)} %pot.1, f32[2,2,32,512]{3,2,1,0:T(8,128)} %get-tuple-element.69.zup, ...), custom_call_target="tpu_custom_call" | custom-call | tf_op jit(solution)/shard_map/pallas_call | solution.py:469
  61.5 0.0 copy-start
  61.5 57.9 %shard_map.61 = (f32[2,22,32,512]{3,2,1,0:T(8,128)S(1)}, f32[32,512]{1,0:T(8,128)S(1)}, f32[8,128]{1,0:T(8,128)}, f32[32,512]{1,0:T(8,128)S(1)}) custom-call(f32[64,32,512]{2,1,0:T(8,128)} %get-tuple-element.54.q_ref, f32[64,32,512]{2,1,0:T(8,128)} %get-tuple-element.55.u_ref, f32[64,32,512]{2,1,0:T(8,128)} %get-tuple-element.56.sum_ref, ...), custom_call_target="tpu_custom_call" | custom-call | tf_op jit(solution)/shard_map/pallas_call | solution.py:497
  119.5 1.3 reduce_max.9
  121.4 0.0 copy-done
  121.4 7.9 %conditional.1 = (f32[16,2,32,512]{3,2,1,0:T(8,128)}) conditional(s32[]{:T(128)} %convert_element_type.32, (f32[32,512]{1,0:T(8,128)S(1)}, f32[32,512]{1,0:T(8,128)S(1)}, f32[64]{0:T(128)S(1)}, f32[64]{0:T(128)S(1)}, f32[64,32,512]{2,1,0:T(8,128)}, /*index=5*/f32[64,32,512]{2,1,0:T(8,128)}, f32[64,32,512]{2,1,0:T(8,128)}) %tuple.14, ...), branch_computations={%region_1.0_spmd, %region_3.0_spmd} | conditional | flops 1605632 | bytes 27459596 | solution.py:565
  121.4 7.9 %branch_1_fun.1 = f32[16,2,32,512]{3,2,1,0:T(8,128)} custom-call(s32[64]{0:T(128)S(1)} %get-tuple-element.36.index, f32[64]{0:T(128)S(1)} %get-tuple-element.37.lam, f32[64]{0:T(128)S(1)} %get-tuple-element.38.weight, f32[1408]{0:T(1024)} %constant.41.clone.1.table, f32[2,22,32,512]{3,2,1,0:T(8,128)S(1)} %get-tuple-element.40.moments, ...), custom_call_target="tpu_custom_call" | custom-call | tf_op jit(solution)/shard_map/cond/branch_1_fun/pallas_call | solution.py:534
  129.4 0.6 copy.19
Async XLA Ops:
  61.5 59.9 %copy-start = (s32[64]{0:T(128)S(1)}, s32[64]{0:T(128)}, u32[]{:S(2)}) copy-start(s32[64]{0:T(128)} %param.7) | copy-start | bytes 772
